TPU v7x, 512 devices: a whole 4x8x8 slice. The times are simulated.
512 devices in a mesh: ctx: 64 (over y, x, core), head: 8 (over z).
Axes of the slice: x: 4, y: 8, z: 8, core: 2. Of those that a mesh axis runs over, the one named last changes fastest.
Arguments:
- head_input: bfloat16 [32768, 5120], P('ctx', 'head'), may hold values from -6 to 6
- bc_input: bfloat16 [32768, 256], P('ctx'), may hold values from -3 to 3
- conv_x: float32 [4, 5120], P(None, 'head'), may hold values from -3 to 3
- conv_bc: float32 [4, 256], replicated, may hold values from -3 to 3
- log_decay: float32 [80, 32768], P('head', 'ctx'), may hold values from -2 to 0
- d_skip: float32 [80], P('head'), may hold values from 0.5 to 2
- gate_z: bfloat16 [32768, 5120], P('ctx', 'head'), may hold values from -400 to 400
- norm_gain: float32 [5120], P('head'), may hold values from 0.1 to 1.9
- w_out: bfloat16 [5120, 2560], P('head'), may hold values from -0.078125 to 0.078125
Outputs:
- layer_out: bfloat16 [32768, 2560], P('ctx', 'head')
All inputs are finite; a program needn't handle non-finite values.
Results may differ from a plain program's by a relative error of at most 0.013.
Values may be sent and summed in bfloat16 or wider, within the bound.
A program may use at most 64 MiB of HBM per device.

v0:
```python
import jax
import jax.numpy as jnp
from jax import lax
from jax.sharding import Mesh
from jax.sharding import PartitionSpec as P

P_SIZE = 64
N = 128
K = 4
CTX = ("ctx_0", "ctx_1", "ctx_2")


def passed_along(block, axis, distance):
    devices = range(lax.axis_size(axis))
    route = [(i - distance, i) for i in devices if i - distance in devices]
    return lax.ppermute(block, axis, route)


def nothing_yet(array, identity):
    return jax.tree.map(
        lambda part, zero: jnp.zeros_like(part) + jnp.asarray(zero, part.dtype), array, identity
    )


def carried_in(array, axes, combine, identity):
    before = start = nothing_yet(array, identity)
    running = array
    for axis in reversed(axes):
        peers, mine = (lax.axis_size(axis), lax.axis_index(axis))
        pieces = jax.tree.map(lambda part: lax.all_gather(part, axis), running)
        inside, running = (start, start)
        for k in range(peers):
            passed = k < mine
            running = combine(running, jax.tree.map(lambda part: part[k], pieces))
            inside = jax.tree.map(lambda new, old: jnp.where(passed, new, old), running, inside)
        before = combine(inside, before)
    return before


def sent_to_all(array, axis):
    copies = jnp.broadcast_to(array, (lax.axis_size(axis), *array.shape))
    return lax.all_to_all(copies, axis, split_axis=0, concat_axis=0, tiled=True)


def taken_together(array, axis):
    everything = sent_to_all(array, axis)
    return jnp.sum(everything, axis=0)


def split_up(array, dim, peers):
    lengths = array.shape
    parts = array.reshape(*lengths[:dim], peers, lengths[dim] // peers, *lengths[dim + 1 :])
    return jnp.moveaxis(parts, dim, 0)


def sum_at_owner(array, axis, dim):
    peers = lax.axis_size(axis)
    parts = lax.all_to_all(split_up(array, dim, peers), axis, 0, 0, tiled=True)
    return jnp.sum(parts.astype(jnp.float32), axis=0)


def causal_apply(local, rim_rows, kernel):
    length = local.shape[0]
    padded = jnp.concatenate([rim_rows.astype(jnp.float32), local.astype(jnp.float32)], axis=0)
    summed = jnp.zeros(local.shape, jnp.float32)
    for tap_index in range(K):
        summed = summed + kernel[tap_index] * padded[tap_index : tap_index + length]
    return summed


def combine_states(earlier, later):
    return (earlier[0] + later[0], jnp.exp(later[0])[:, None, None] * earlier[1] + later[1])


def shards(head_input, bc_input, conv_x, conv_bc, log_decay, d_skip, gate_z, norm_gain, w_out):
    margin = K - 1
    rim_x, rim_bc = passed_along((head_input[-margin:], bc_input[-margin:]), CTX, 1)
    xconv = jax.nn.silu(causal_apply(head_input, rim_x, conv_x)).astype(jnp.bfloat16)
    bc_conv = jax.nn.silu(causal_apply(bc_input, rim_bc, conv_bc)).astype(jnp.bfloat16)
    length = head_input.shape[0]
    heads_local = log_decay.shape[0]
    x_heads = xconv.reshape(length, heads_local, P_SIZE)
    write_keys = bc_conv[:, :N]
    read_keys = bc_conv[:, N:]
    cumulative = jnp.cumsum(log_decay, axis=1)
    gram_matrix = jnp.dot(read_keys, write_keys.T, preferred_element_type=jnp.float32)
    position = jnp.arange(length)
    lower_mask = position[:, None] >= position[None, :]
    spread = jnp.minimum(cumulative[:, :, None] - cumulative[:, None, :], 0.0)
    mixing = jnp.where(lower_mask[None], gram_matrix[None] * jnp.exp(spread), 0.0).astype(
        jnp.bfloat16
    )
    y_local = jnp.einsum("hts,shp->thp", mixing, x_heads, preferred_element_type=jnp.float32)
    head_float = x_heads.astype(jnp.float32)
    weights = jnp.exp(cumulative[:, -1:] - cumulative)
    scaled = (head_float * weights.T[:, :, None]).astype(jnp.bfloat16)
    block_state = jnp.einsum("shp,sn->hpn", scaled, write_keys, preferred_element_type=jnp.float32)
    block_log = cumulative[:, -1]
    identity = (jnp.zeros(block_log.shape, jnp.float32), jnp.zeros(block_state.shape, jnp.float32))
    prefix = carried_in((block_log, block_state), CTX, combine_states, identity)
    incoming = prefix[1]
    y_state = (
        jnp.einsum(
            "tn,hpn->thp", read_keys.astype(jnp.float32), incoming, precision=lax.Precision.HIGHEST
        )
        * jnp.exp(cumulative).T[:, :, None]
    )
    ssm_out = (y_local + y_state + d_skip[None, :, None] * head_float).reshape(
        length, heads_local * P_SIZE
    )
    gated = ssm_out * jax.nn.silu(gate_z.astype(jnp.float32))
    local_squares = jnp.sum(gated * gated, axis=1)
    mean_square = taken_together(local_squares, "head") / (gated.shape[1] * lax.axis_size("head"))
    normed = (gated * lax.rsqrt(mean_square + 1e-05)[:, None] * norm_gain[None, :]).astype(
        jnp.bfloat16
    )
    terms = jnp.dot(normed, w_out, preferred_element_type=jnp.float32)
    layer_out = sum_at_owner(terms.astype(jnp.bfloat16), "head", 1).astype(jnp.bfloat16)
    return layer_out


def solution(mesh):
    split = Mesh(
        mesh.devices.reshape(8, 4, 2, mesh.shape["head"]), ("ctx_0", "ctx_1", "ctx_2", "head")
    )
    return jax.shard_map(
        shards,
        mesh=split,
        in_specs=(
            P(CTX, "head"),
            P(CTX, None),
            P(None, "head"),
            P(),
            P("head", CTX),
            P("head"),
            P(CTX, "head"),
            P("head"),
            P("head", None),
        ),
        out_specs=P(CTX, "head"),
        check_vma=False,
    )
```

profile of v0, /device:TPU:6, one launch (start us, length us, event | category | flops | bytes accessed | tf_op | source)
XLA Modules:
  0.0 231.0 jit_solution(16889261542433611290)
XLA Ops:
  6.5 0.9 slice.149
  7.4 2.0 collective-permute-start
  9.4 1.3 slice.157
  10.7 3.5 %collective-permute-start.1 = (bf16[3,256]{1,0:T(4,128)(2,1)}, bf16[3,256]{1,0:T(4,128)(2,1)}, u32[]{:S(2)}, u32[]{:S(2)}) collective-permute-start(bf16[3,256]{1,0:T(4,128)(2,1)} %slice.157), channel_id=1, source_target_pairs={{0,8},{8,16},{16,24},{24,32},{32,40},{40,48},{48,56},{56,64},{64,7... | collective-permute-start | bytes 4616 | tf_op jit(solution)/shard_map/ppermute | solution.py:16
  14.2 0.8 reshape.229
  15.0 1.2 reduce-window.6
  16.2 0.2 slice_reduce_fusion
  16.5 1.4 fusion.143
  18.0 0.2 slice_reduce_fusion.1
  18.1 0.7 exponential_bitcast_fusion.1
  18.8 1.2 dynamic-slice.1
  20.1 1.3 dynamic-slice
  22.6 0.6 broadcast.124
  23.1 1.3 dynamic-update-slice
  24.5 2.6 %all-reduce = f32[20]{0:T(128)S(1)} all-reduce(f32[20]{0:T(128)} %dynamic-update-slice), channel_id=2, replica_groups=mesh['ctx_0'=8,'ctx_1'=4,'ctx_2'=2,'head'=8] {'ctx_2'}, use_global_device_ids=true, to_apply=%add | all-reduce | flops 20 | bytes 160
  27.0 0.7 fusion.137
  27.7 0.6 copy-done.14
  28.3 0.9 slice_reduce_fusion.5
  29.2 1.2 convert_element_type.40
  30.5 0.7 convert_element_type.42
  31.2 0.3 multiply_convert_fusion.3
  31.5 0.7 convert_element_type.39
  32.2 1.6 multiply_convert_fusion.1
  33.8 2.2 copy.37
  36.0 1.4 fusion.18
  37.5 2.3 all-gather.1
  39.8 0.8 copy-done.2
  40.6 0.8 bitcast_add_fusion.4
  41.5 10.6 %all-reduce.1 = f32[40]{0:T(128)S(1)} all-reduce(f32[40]{0:T(128)S(1)} %copy-done.15), channel_id=4, replica_groups=mesh['ctx_0'=8,'ctx_1'=4,'ctx_2'=2,'head'=8] {'ctx_1'}, use_global_device_ids=true, to_apply=%add.1 | all-reduce | flops 40 | bytes 320
  52.2 0.6 fusion.136
  52.8 0.6 fusion.138
  53.4 21.9 %all-gather.7.cloned.1.call-done = f32[4,10,64,128]{3,2,1,0:T(8,128)} async-done(((f32[1,10,64,128]{3,2,1,0:T(8,128)}), f32[4,10,64,128]{3,2,1,0:T(8,128)}) %all-gather.7.cloned.1.call-update) | async-done | bytes 1310736 | tf_op jit(solution)/shard_map/all_gather | solution.py:30
  75.3 2.2 multiply_add_fusion
  77.5 16.3 %all-gather.3 = f32[8,1,10]{2,1,0:T(1,128)S(1)} all-gather(f32[1,1,10]{2,1,0:T(1,128)S(1)} %copy-done.12), channel_id=1, replica_groups=mesh['ctx_0'=8,'ctx_1'=4,'ctx_2'=2,'head'=8] {'ctx_0'}, dimensions={0}, use_global_device_ids=true | all-gather | bytes 360 | tf_op jit(solution)/shard_map/all_gather | solution.py:30
  93.8 0.1 iota_compare_fusion
  93.8 1.1 exponential_bitcast_fusion.2
  95.0 0.6 fusion.135
  95.6 0.3 fusion.120
  95.9 4.2 %fusion.4 = f32[512,10,64]{0,2,1:T(8,128)} fusion(bf16[512,10,64]{0,2,1:T(8,128)(2,1)S(1)} %bitcast.158, f32[10,512]{1,0:T(8,128)S(1)} %bitcast.162, f32[512,512]{1,0:T(8,128)S(1)} %fusion.120, pred[512,512]{1,0:T(8,128)(4,1)S(1)} %iota_compare_fusion), kind=kOutput, calls=%fused_computation.13 | convolution fusion | flops 348651520 | bytes 3297280 | tf_op jit(solution)/shard_map/hts,shp->thp/dot_general | solution.py:93
  100.1 23.5 %all-gather.9.cloned.1.call-done = f32[8,10,64,128]{3,2,1,0:T(8,128)} async-done(((f32[1,10,64,128]{3,2,1,0:T(8,128)}), f32[8,10,64,128]{3,2,1,0:T(8,128)}) %all-gather.9.cloned.1.call-update) | async-done | bytes 2621456 | tf_op jit(solution)/shard_map/all_gather | solution.py:30
  123.6 5.3 %fusion.3 = f32[512,10,64]{0,2,1:T(8,128)} fusion(f32[512,10,64]{0,2,1:T(8,128)} %fusion.4, bf16[512,10,64]{0,2,1:T(8,128)(2,1)} %bitcast.157, f32[10]{0:T(128)} %param.14, f32[512,10]{0,1:T(8,128)} %get-tuple-element.13, f32[8,10,64,128]{3,2,1,0:T(8,128)} %all-gather.9.cloned.1.call-done, f32[4,10,64,128]{3,2,1,0:T(8,128)} %all-gather.7.cloned.1.call-done, ...), kind=kOutput, calls=%fused_computation.12 | convolution fusion | flops 508477440 | bytes 8018454 | tf_op jit(solution)/shard_map/tn,hpn->thp/dot_general | solution.py:103
  128.9 2.8 %copy.40 = f32[512,640]{1,0:T(8,128)} copy(f32[512,640]{0,1:T(8,128)} %bitcast.159) | data formatting | bytes 2621440 | tf_op jit(solution)/shard_map/reshape | solution.py:108
  131.7 2.0 multiply_reduce_fusion
  133.8 14.9 %all_to_all.11 = f32[8,1,512]{2,1,0:T(1,128)S(1)} all-to-all(f32[8,1,512]{2,1,0:T(1,128)S(1)} %broadcast_in_dim.16), channel_id=1, replica_groups=mesh['ctx_0'=8,'ctx_1'=4,'ctx_2'=2,'head'=8] {'head'}, dimensions={0} | all-to-all | bytes 32768 | tf_op jit(solution)/shard_map/all_to_all | solution.py:42
  148.8 5.5 %convolution_convert_fusion = bf16[512,2560]{1,0:T(8,128)(2,1)} fusion(bf16[640,2560]{1,0:T(8,128)(2,1)S(1)} %copy-done, f32[640]{0:T(1024)S(1)} %copy-done.13, f32[512]{0:T(512)S(1)} %add_rsqrt_fusion, f32[512,640]{1,0:T(8,128)} %copy.40, bf16[512,640]{1,0:T(8,128)(2,1)} %param.15), kind=kOutput, calls=%fused_computation.3 | convolution fusion | flops 1681981440 | bytes 7868928 | tf_op jit(solution)/shard_map/dot_general | solution.py:117
  154.3 4.4 %copy.42 = bf16[512,2560]{0,1:T(8,128)(2,1)} copy(bf16[512,2560]{1,0:T(8,128)(2,1)} %convolution_convert_fusion) | data formatting | bytes 5242880 | tf_op jit(solution)/shard_map/convert_element_type | solution.py:118
  158.7 62.5 %all_to_all.12 = bf16[8,512,320]{1,2,0:T(8,128)(2,1)} all-to-all(bf16[8,512,320]{1,2,0:T(8,128)(2,1)} %bitcast.155), channel_id=1, replica_groups=mesh['ctx_0'=8,'ctx_1'=4,'ctx_2'=2,'head'=8] {'head'}, dimensions={0} | all-to-all | bytes 5242880 | tf_op jit(solution)/shard_map/all_to_all | solution.py:58
  221.2 2.9 %reduce_sum.32 = bf16[512,320]{0,1:T(8,128)(2,1)} reduce(bf16[8,512,320]{1,2,0:T(8,128)(2,1)} %all_to_all.12, bf16[]{:T(256)} %constant.52.clone.1), dimensions={0}, to_apply=%region_4.5 | reduce | flops 1146880 | bytes 2949122 | tf_op jit(solution)/shard_map/reduce_sum | solution.py:59
  (48 shorter events, 0.4 us)
Async XLA Ops:
  6.5 142.2 %copy-start = (bf16[640,2560]{1,0:T(8,128)(2,1)S(1)}, bf16[640,2560]{1,0:T(8,128)(2,1)}, u32[]{:S(2)}) copy-start(bf16[640,2560]{1,0:T(8,128)(2,1)} %param.17) | copy-start | bytes 9830404
  6.5 68.7 %all-gather.7.cloned.1.call-start = ((), (), s32[]{:S(2)}) async-start(), calls=%async_computation.2 | async-start | bytes 1638400 | tf_op jit(solution)/shard_map/all_gather | solution.py:30
  7.4 24.1 %collective-permute-start = (bf16[3,640]{1,0:T(4,128)(2,1)S(1)}, bf16[3,640]{1,0:T(4,128)(2,1)}, u32[]{:S(2)}, u32[]{:S(2)}) collective-permute-start(bf16[3,640]{1,0:T(4,128)(2,1)S(1)} %slice.149), channel_id=1, source_target_pairs={{0,8},{8,16},{16,24},{24,32},{32,40},{40,48},{48,56},{56,64},{64,7... | collective-permute-start | bytes 11528 | tf_op jit(solution)/shard_map/ppermute | solution.py:16
  10.7 19.7 %collective-permute-start.1 = (bf16[3,256]{1,0:T(4,128)(2,1)}, bf16[3,256]{1,0:T(4,128)(2,1)}, u32[]{:S(2)}, u32[]{:S(2)}) collective-permute-start(bf16[3,256]{1,0:T(4,128)(2,1)} %slice.157), channel_id=1, source_target_pairs={{0,8},{8,16},{16,24},{24,32},{32,40},{40,48},{48,56},{56,64},{64,7... | collective-permute-start | bytes 4616 | tf_op jit(solution)/shard_map/ppermute | solution.py:16
  16.4 14.0 %copy-start.3 = (bf16[512,256]{1,0:T(8,128)(2,1)S(1)}, bf16[512,256]{1,0:T(8,128)(2,1)}, u32[]{:S(2)}) copy-start(bf16[512,256]{1,0:T(8,128)(2,1)} %param.10) | copy-start | bytes 786436
  16.5 1.6 copy-start.4
  27.7 0.6 copy-start.14
  29.2 2.0 copy-start.6
  29.2 1.9 copy-start.7
  29.2 1.9 copy-start.8
  36.0 4.6 %copy-start.10 = (f32[10]{0:T(128)S(1)}, f32[10]{0:T(128)}, u32[]{:S(2)}) copy-start(f32[10]{0:T(128)} %get-tuple-element.32) | copy-start | bytes 124
  36.0 4.6 %copy-start.11 = (f32[10]{0:T(128)S(1)}, f32[10]{0:T(128)}, u32[]{:S(2)}) copy-start(f32[10]{0:T(128)} %get-tuple-element.33) | copy-start | bytes 124
  37.5 4.1 %copy-start.15 = (f32[40]{0:T(128)S(1)}, f32[40]{0:T(128)}, u32[]{:S(2)}) copy-start(f32[40]{0:T(128)} %copy-done.14) | copy-start | bytes 484
  39.8 0.8 copy-start.2
  41.5 82.1 %all-gather.9.cloned.1.call-start = ((), (), s32[]{:S(2)}) async-start(), calls=%async_computation.3 | async-start | bytes 2949120 | tf_op jit(solution)/shard_map/all_gather | solution.py:30
  53.4 24.1 %copy-start.12 = (f32[1,1,10]{2,1,0:T(1,128)S(1)}, f32[1,1,10]{2,1,0:T(1,128)}, u32[]{:S(2)}) copy-start(f32[1,1,10]{2,1,0:T(1,128)} %get-tuple-element.26) | copy-start | bytes 124
  77.5 18.4 %copy-start.1 = (bf16[512,640]{0,1:T(8,128)(2,1)S(1)}, bf16[512,640]{0,1:T(8,128)(2,1)}, u32[]{:S(2)}) copy-start(bf16[512,640]{0,1:T(8,128)(2,1)} %copy.37) | copy-start | bytes 1966084
  77.5 18.4 %copy-start.5 = (f32[2,8,4,128]{3,1,2,0:T(8,128)S(1)}, f32[2,8,4,128]{3,1,2,0:T(8,128)}, u32[]{:S(2)}) copy-start(f32[2,8,4,128]{3,1,2,0:T(8,128)} %copy-done.4) | copy-start | bytes 98308
  95.9 27.7 %copy-start.9 = (f32[10]{0:T(128)S(1)}, f32[10]{0:T(128)}, u32[]{:S(2)}) copy-start(f32[10]{0:T(128)} %get-tuple-element.30) | copy-start | bytes 124
  131.7 17.0 %copy-start.13 = (f32[640]{0:T(1024)S(1)}, f32[640]{0:T(1024)}, u32[]{:S(2)}) copy-start(f32[640]{0:T(1024)} %param.16) | copy-start | bytes 7684
Sparse Core Ops, SparseCore 0:
  41.6 33.6 all-gather.6
  77.6 45.9 all-gather.8
where the time goes:
time: 232 us; the launch traced here: 231 us
  blocking collectives  109 us (47%)
  waiting for transfers between devices  45.4 us (20%)
  local copies, waits for them, and re-layouts  22.1 us (10%)
  other arithmetic  17.1 us (7%)
  matrix products  16.7 us (7%)
  between operations  14.9 us (6%)
  starting transfers between devices  5.58 us (2%)
    all_to_all x1, blocking collectives, sum_at_owner(): parts = lax.all_to_all(split_up(array, dim, peers), axis, 0, 0, tiled=True)  62.5 us
    all_gather x2, waiting for transfers between devices, carried_in(): pieces = jax.tree.map(lambda part: lax.all_gather(part, axis), running)  45.4 us
    all_gather x2, blocking collectives, carried_in(): pieces = jax.tree.map(lambda part: lax.all_gather(part, axis), running)  18.5 us
    all_to_all x1, blocking collectives, sent_to_all(): return lax.all_to_all(copies, axis, split_axis=0, concat_axis=0, tiled=True)  14.9 us
    unnamed x2, blocking collectives  13.2 us
    unnamed x39, local copies, waits for them, and re-layouts  5.92 us
    ppermute x2, starting transfers between devices, passed_along(): return lax.ppermute(block, axis, route)  5.53 us
    dot_general x1, matrix products, shards(): terms = jnp.dot(normed, w_out, preferred_element_type=jnp.float32)  5.51 us
  transfers between devices with their start and end apart: 4, of which 2 were waited for; matrix products, arithmetic and copies ran while one was open for 9% of the time, Pallas kernels for 0%

commit v1 on v0

v1 whole, which is shorter than its diff:
```python
import functools

import jax
import jax.numpy as jnp
from jax import lax
from jax.experimental import pallas as pl
from jax.experimental.pallas import tpu as pltpu
from jax.sharding import Mesh
from jax.sharding import PartitionSpec as P

F32 = jnp.float32
BF16 = jnp.bfloat16
MESH = pl.DeviceIdType.MESH
N = 128
K = 4
LANES = 128
ROWS = 64
SUBS = 4
CTX = ("y", "x", "c")


def split_three(value):
    high = value.astype(BF16)
    rest = value - high.astype(F32)
    middle = rest.astype(BF16)
    low = (rest - middle.astype(F32)).astype(BF16)
    return high, middle, low


def silu(value):
    small = jnp.exp(-jnp.abs(value))
    return value * jnp.where(value >= 0, 1.0, small) / (1.0 + small)


def dot(a, b, dims):
    return lax.dot_general(a, b, (dims, ((), ())), preferred_element_type=F32)


def iota(shape, dim):
    return lax.broadcasted_iota(jnp.int32, shape, dim)


def remote(source, target, send_sem, recv_sem, device):
    return pltpu.make_async_remote_copy(
        src_ref=source,
        dst_ref=target,
        send_sem=send_sem,
        recv_sem=recv_sem,
        device_id=device,
        device_id_type=MESH,
    )


def kernel(
    sizes,
    x_hbm, bc_hbm, cx_hbm, cbc_hbm, ld_hbm, d_hbm, gate_hbm, gain_hbm, w_hbm,
    out_ref,
    x_in, bc_in, cx, cbc, ld, d_skip, gate, gain, w,
    load_sem,
    halo_x, halo_bc, halo_send, halo_recv,
    xf, bcf, xc, bcc, crow, cum, cum2, gram, scaled, state,
    decay_row, decay_send, decay_recv,
    total_row, total_send, total_recv,
    row_buf, row_send, row_recv, prefix,
    y_buf, y_send, y_recv,
    c_out, carried, c_send, c_recv,
    ya, yb, u, sq_part,
    sq_buf, sq_send, sq_recv,
    chunks, long_out, short_out, long_in, short_in,
    long_send, long_recv, short_send, short_recv,
    rstd,
):
    ny, nx, nc, nz = sizes
    nj = nx * nc
    y, x, c, z = (lax.axis_index(name) for name in ("y", "x", "c", "z"))
    j = x * nc + c
    flat = y * nj + j
    slab = N // nj
    heads, length = ld.shape
    width = x_in.shape[1]
    pairs = width // LANES

    loads = [
        pltpu.make_async_copy(source, target, load_sem.at[i])
        for i, (source, target) in enumerate(
            [
                (ld_hbm, ld), (x_hbm, x_in), (bc_hbm, bc_in), (cx_hbm, cx), (cbc_hbm, cbc),
                (d_hbm, d_skip), (gate_hbm, gate), (gain_hbm, gain), (w_hbm, w),
            ]
        )
    ]
    for load in loads:
        load.start()

    def member(index):
        return {"x": lax.div(index, nc), "c": lax.rem(index, nc)}

    def at(index):
        return {"y": lax.div(index, nj), **member(lax.rem(index, nj))}

    after = at(lax.rem(flat + 1, ny * nj))
    ahead = at(lax.rem(flat + ny * nj - 1, ny * nj))

    barrier = pltpu.get_barrier_semaphore()

    def greet(device):
        pl.semaphore_signal(barrier, inc=1, device_id=device, device_id_type=MESH)

    greet(after)
    greet(ahead)
    for k in range(1, ny):
        greet({"y": lax.rem(y + k, ny)})
    for k in range(1, nz):
        greet({"z": lax.rem(z + k, nz)})
    for k in range(1, nj):
        greet(member(lax.rem(j + k, nj)))

    loads[0].wait()
    padded = jnp.concatenate([ld[...], jnp.zeros((16 - heads, length), F32)], axis=0)
    upper = (iota((length, length), 0) <= iota((length, length), 1)).astype(BF16)
    three = dot(jnp.concatenate(split_three(padded), axis=0), upper, ((1,), (0,)))
    rows = three[0:16] + (three[16:32] + three[32:48])
    for h in range(heads):
        crow[h] = rows[h : h + 1]
    stacked = jnp.concatenate(split_three(rows), axis=0)
    pick = (iota((48, width), 0) & 15) == lax.shift_right_logical(iota((48, width), 1), 6)
    cum[...] = dot(stacked, pick.astype(BF16), ((0,), (0,)))
    wide = heads * LANES
    pick2 = (iota((48, wide), 0) & 15) == lax.shift_right_logical(iota((48, wide), 1), 7)
    cum2[...] = dot(stacked, pick2.astype(BF16), ((0,), (0,)))
    decay_row[j] = cum[length - 1 : length, :]

    loads[1].wait()
    loads[2].wait()
    pl.semaphore_wait(barrier, 2 + (ny - 1) + (nz - 1) + (nj - 1))

    tail = pl.ds(length - 16, 16)
    halos = [
        remote(x_in.at[tail], halo_x, halo_send.at[0], halo_recv.at[0], after),
        remote(bc_in.at[tail], halo_bc, halo_send.at[1], halo_recv.at[1], after),
    ]

    @pl.when(flat < ny * nj - 1)
    def _():
        for copy in halos:
            copy.start()

    decays = []
    for k in range(1, nj):
        other = lax.rem(j + k, nj)
        copy = remote(
            decay_row.at[j], decay_row.at[j], decay_send.at[k], decay_recv.at[j], member(other)
        )
        copy.start()
        decays.append(copy)

    loads[3].wait()
    loads[4].wait()
    xf[0:8, :] = jnp.zeros((8, width), F32)
    bcf[0:8, :] = jnp.zeros((8, 2 * N), F32)

    def widen(i, _):
        r = pl.multiple_of(i * ROWS, ROWS)
        xf[pl.ds(r + 8, ROWS), :] = x_in[pl.ds(r, ROWS), :].astype(F32)
        bcf[pl.ds(r + 8, ROWS), :] = bc_in[pl.ds(r, ROWS), :].astype(F32)
        return 0

    lax.fori_loop(0, length // ROWS, widen, 0)

    def filtered(source, taps, r):
        block = source[pl.ds(r, ROWS + 8), :]
        total = taps[K - 1 : K, :] * block[8:]
        for tap in range(K - 1):
            total = total + taps[tap : tap + 1, :] * pltpu.roll(block, K - 1 - tap, 0)[8:]
        return silu(total).astype(BF16)

    def convolve(i, _):
        r = pl.multiple_of(i * ROWS, ROWS)
        here = pl.ds(r, ROWS)
        conv = filtered(xf, cx, r)
        xc[here, :] = conv
        bcc[here, :] = filtered(bcf, cbc, r)
        weight = jnp.exp(cum[length - 1 : length, :] - cum[here, :])
        scaled[here, :] = (conv.astype(F32) * weight).astype(BF16)
        return 0

    lax.fori_loop(1, length // ROWS, convolve, 0)

    @pl.when(flat > 0)
    def _():
        for copy in halos:
            copy.wait_recv()
        xf[0:8, :] = halo_x[8:16, :].astype(F32)
        bcf[0:8, :] = halo_bc[8:16, :].astype(F32)

    convolve(0, 0)

    state[...] = dot(bcc[:, 0:N], scaled[...], ((0,), (0,))).astype(BF16)
    row_buf[j] = state[pl.ds(pl.multiple_of(j * slab, slab), slab), :]
    sent = []
    for k in range(1, nj):
        other = lax.rem(j + k, nj)
        copy = remote(
            state.at[pl.ds(pl.multiple_of(other * slab, slab), slab)],
            row_buf.at[j],
            row_send.at[k],
            row_recv.at[j],
            member(other),
        )
        copy.start()
        sent.append(copy)

    for k in range(1, nj):
        other = lax.rem(j + k, nj)
        remote(
            decay_row.at[other], decay_row.at[other], decay_send.at[k], decay_recv.at[other],
            member(other),
        ).wait_recv()
    whole = decay_row[0]
    for i in range(1, nj):
        whole = whole + decay_row[i]
    total_row[y] = whole
    totals = []
    for k in range(1, ny):
        copy = remote(
            total_row.at[y], total_row.at[y], total_send.at[k], total_recv.at[y],
            {"y": lax.rem(y + k, ny)},
        )
        copy.start()
        totals.append(copy)

    gram[...] = dot(bcc[:, N : 2 * N], bcc[:, 0:N], ((1,), (1,)))
    left = iota((LANES, LANES), 1) < 64
    causal = iota((LANES, LANES), 0) >= iota((LANES, LANES), 1)
    loads[5].wait()

    def local_pair(i, _):
        lanes = pl.ds(pl.multiple_of(i * LANES, LANES), LANES)
        for block in range(length // LANES):
            t = slice(block * LANES, (block + 1) * LANES)
            results = []
            for side in range(2):
                h = 2 * i + side
                here = cum2[t, pl.ds(pl.multiple_of(h * LANES, LANES), LANES)]
                parts = []
                for other in range(block + 1):
                    s = slice(other * LANES, (other + 1) * LANES)
                    spread = here - crow[h, :, s]
                    if other == block:
                        part = jnp.where(causal, gram[t, s] * jnp.exp(jnp.minimum(spread, 0.0)), 0.0)
                    else:
                        part = gram[t, s] * jnp.exp(spread)
                    parts.append(part.astype(BF16))
                mixing = parts[0] if block == 0 else jnp.concatenate(parts, axis=1)
                results.append(dot(mixing, xc[0 : (block + 1) * LANES, lanes], ((1,), (0,))))
            skip = jnp.where(left, d_skip[2 * i], d_skip[2 * i + 1])
            ya[t, lanes] = jnp.where(left, results[0], results[1]) + skip * xc[t, lanes].astype(F32)
        return 0

    lax.fori_loop(0, 2, local_pair, 0)

    for k in range(1, nj):
        other = lax.rem(j + k, nj)
        remote(
            row_buf.at[other], row_buf.at[other], row_send.at[k], row_recv.at[other], member(other)
        ).wait_recv()
    running = jnp.zeros((slab, width), F32)
    for i in range(nj):
        prefix[i] = running
        running = jnp.exp(decay_row[i]) * running + row_buf[i].astype(F32)
    y_buf[y] = running.astype(BF16)
    for k in range(1, ny):

        @pl.when(y + k < ny)
        def _(k=k):
            remote(
                y_buf.at[y], y_buf.at[y], y_send.at[k], y_recv.at[y], {"y": lax.rem(y + k, ny)}
            ).start()

    lax.fori_loop(2, pairs, local_pair, 0)

    loads[6].wait()

    def gates(i, _):
        here = pl.ds(pl.multiple_of(i * ROWS, ROWS), ROWS)
        factor = silu(gate[here, :].astype(F32))
        ya[here, :] = ya[here, :] * factor
        yb[here, :] = jnp.exp(cum[here, :]) * factor
        return 0

    lax.fori_loop(0, length // ROWS, gates, 0)

    for k in range(1, ny):
        other = lax.rem(y + k, ny)
        remote(
            total_row.at[other], total_row.at[other], total_send.at[k], total_recv.at[other],
            {"y": other},
        ).wait_recv()
    for k in range(1, ny):

        @pl.when(y >= k)
        def _(k=k):
            other = lax.rem(y - k + ny, ny)
            remote(
                y_buf.at[other], y_buf.at[other], y_send.at[k], y_recv.at[other], {"y": other}
            ).wait_recv()

    def earlier(i, total):
        return jnp.exp(total_row[i]) * total + y_buf[i].astype(F32)

    base = lax.fori_loop(0, y, earlier, jnp.zeros((slab, width), F32))
    fade = jnp.zeros((1, width), F32)
    for i in range(nj):
        c_out[i] = (jnp.exp(fade) * base + prefix[i]).astype(BF16)
        fade = fade + decay_row[i]
    mine = pl.ds(pl.multiple_of(j * slab, slab), slab)
    carried[mine, :] = c_out[j]
    returned = []
    for k in range(1, nj):
        other = lax.rem(j + k, nj)
        copy = remote(c_out.at[other], carried.at[mine], c_send.at[k], c_recv.at[j], member(other))
        copy.start()
        returned.append(copy)
    loads[7].wait()
    loads[8].wait()
    for k in range(1, nj):
        other = lax.rem(j + k, nj)
        theirs = carried.at[pl.ds(pl.multiple_of(other * slab, slab), slab)]
        remote(theirs, theirs, c_send.at[k], c_recv.at[other], member(other)).wait_recv()

    def finish(i, _):
        here = pl.ds(pl.multiple_of(i * LANES, LANES), LANES)
        from_state = dot(bcc[here, N : 2 * N], carried[...], ((1,), (0,)))
        gated = ya[here, :] + yb[here, :] * from_state
        u[here, :] = (gated * gain[...]).astype(BF16)
        square = gated * gated
        total = square[:, 0:LANES]
        for part in range(1, pairs):
            total = total + square[:, part * LANES : (part + 1) * LANES]
        sq_part[here, :] = total
        return 0

    lax.fori_loop(0, length // LANES, finish, 0)

    ts = length // SUBS
    quarter = ts // 4
    half = iota((quarter, LANES), 1) < 64

    def project(p):
        col = pl.multiple_of(p * 5 * LANES, LANES)
        for begin, dest in ((0, 2 * p), (3 * LANES, 2 * p + 1)):
            part = dot(u[...], w[:, pl.ds(col + begin, 2 * LANES)], ((1,), (0,)))
            for q in range(SUBS):
                chunks[dest, q, 0:ts, :] = part[q * ts : (q + 1) * ts].astype(BF16)
        middle = dot(u[...], w[:, pl.ds(col + 2 * LANES, LANES)], ((1,), (0,)))
        turned = pltpu.roll(middle, 64, 1)
        for q in range(SUBS):
            m = [middle[q * ts + g * quarter : q * ts + (g + 1) * quarter] for g in range(4)]
            r = [turned[q * ts + g * quarter : q * ts + (g + 1) * quarter] for g in range(4)]
            even = [jnp.where(half, m[g], r[g + 1]) for g in (0, 2)]
            odd = [jnp.where(half, r[g], m[g + 1]) for g in (0, 2)]
            chunks[2 * p, q, ts : ts + quarter, :] = jnp.concatenate(even, axis=1).astype(BF16)
            chunks[2 * p + 1, q, ts : ts + quarter, :] = jnp.concatenate(odd, axis=1).astype(BF16)

    sign = 1 - 2 * c
    n_long = nz // 2
    n_short = n_long - 1

    def towards(offset):
        return lax.rem(z + offset * sign + 2 * nz, nz)

    def long_copy(source, step, q):
        return remote(
            source, long_in.at[step, q], long_send.at[step, q], long_recv.at[step, q],
            {"z": towards(1)},
        )

    def short_copy(source, step, q):
        return remote(
            source, short_in.at[step, q], short_send.at[step, q], short_recv.at[step, q],
            {"z": towards(-1)},
        )

    half_nz = nz // 2
    first = lax.div(towards(n_long), 2)

    def pair_at(offset):
        return lax.rem(first + offset * sign + 2 * half_nz, half_nz)

    def start_long(q, _):
        long_copy(chunks.at[towards(n_long), q], 0, q).start()
        return 0

    def start_short(q, _):
        short_copy(chunks.at[towards(-n_short), q], 0, q).start()
        return 0

    order = [0, 1, -1, 2][:half_nz] if half_nz > 2 else list(range(half_nz))
    project(pair_at(order[0]))
    lax.fori_loop(0, SUBS, start_long, 0)
    if half_nz > 1:
        project(pair_at(order[1]))
    if n_short:
        lax.fori_loop(0, SUBS, start_short, 0)

    squares = jnp.zeros((16, length), F32)
    for piece in split_three(sq_part[...]):
        squares = squares + dot(jnp.ones((16, LANES), BF16), piece, ((1,), (1,)))
    sq_buf[z] = squares[0:1, :]
    shared = []
    for k in range(1, nz):
        copy = remote(
            sq_buf.at[z], sq_buf.at[z], sq_send.at[k], sq_recv.at[z], {"z": lax.rem(z + k, nz)}
        )
        copy.start()
        shared.append(copy)
    for offset in order[2:]:
        project(pair_at(offset))

    for step in range(1, n_long):

        def relay(q, _, step=step):
            long_copy(long_in.at[step - 1, q], step - 1, q).wait_recv()
            long_out[step - 1, q] = (
                long_in[step - 1, q].astype(F32) + chunks[towards(n_long - step), q].astype(F32)
            ).astype(BF16)
            long_copy(long_out.at[step - 1, q], step, q).start()
            if step < n_short:
                short_copy(short_in.at[step - 1, q], step - 1, q).wait_recv()
                short_out[step - 1, q] = (
                    short_in[step - 1, q].astype(F32)
                    + chunks[towards(step - n_short), q].astype(F32)
                ).astype(BF16)
                short_copy(short_out.at[step - 1, q], step, q).start()
            return 0

        lax.fori_loop(0, SUBS, relay, 0)

    for k in range(1, nz):
        other = lax.rem(z + k, nz)
        remote(sq_buf.at[other], sq_buf.at[other], sq_send.at[k], sq_recv.at[other], {"z": other}).wait_recv()
    summed = sq_buf[0]
    for i in range(1, nz):
        summed = summed + sq_buf[i]
    high, middle, low = split_three(summed)
    which = iota((16, length), 0)
    table = jnp.where(
        which == 0,
        high.astype(F32),
        jnp.where(which == 1, middle.astype(F32), jnp.where(which == 2, low.astype(F32), 0.0)),
    ).astype(BF16)
    spread = dot(table, jnp.ones((16, LANES), BF16), ((0,), (0,)))
    rstd[...] = lax.rsqrt(spread * (1.0 / (width * nz)) + 1e-5)

    def deliver(q, _):
        long_copy(long_in.at[n_long - 1, q], n_long - 1, q).wait_recv()
        total = chunks[z, q].astype(F32) + long_in[n_long - 1, q].astype(F32)
        if n_short:
            short_copy(short_in.at[n_short - 1, q], n_short - 1, q).wait_recv()
            total = total + short_in[n_short - 1, q].astype(F32)
        base = pl.multiple_of(q * ts, ts)
        here = pl.ds(base, ts)
        scale = rstd[here, :]
        a0 = total[0:ts, 0:LANES] * scale
        a1 = total[0:ts, LANES : 2 * LANES] * scale
        b0 = total[ts : ts + quarter, 0:LANES]
        b1 = total[ts : ts + quarter, LANES : 2 * LANES]
        b = jnp.concatenate([b0, pltpu.roll(b0, 64, 1), b1, pltpu.roll(b1, 64, 1)], axis=0) * scale

        @pl.when(lax.rem(z, 2) == 0)
        def _():
            out_ref[here, 0:LANES] = a0.astype(BF16)
            out_ref[here, LANES : 2 * LANES] = a1.astype(BF16)
            out_ref[here, 2 * LANES : 2 * LANES + 64] = b[:, 0:64].astype(BF16)

        @pl.when(lax.rem(z, 2) == 1)
        def _():
            r0 = pltpu.roll(a0, 64, 1)
            r1 = pltpu.roll(a1, 64, 1)
            low_half = iota((ts, LANES), 1) < 64
            out_ref[here, 0:LANES] = jnp.where(low_half, b, r0).astype(BF16)
            out_ref[here, LANES : 2 * LANES] = jnp.where(low_half, r0, r1).astype(BF16)
            out_ref[here, 2 * LANES : 2 * LANES + 64] = r1[:, 0:64].astype(BF16)

        return 0

    lax.fori_loop(0, SUBS, deliver, 0)

    @pl.when(flat < ny * nj - 1)
    def _():
        for copy in halos:
            copy.wait_send()

    for copy in decays + totals + sent + returned + shared:
        copy.wait_send()
    for k in range(1, ny):

        @pl.when(y + k < ny)
        def _(k=k):
            remote(
                y_buf.at[y], y_buf.at[y], y_send.at[k], y_recv.at[y], {"y": lax.rem(y + k, ny)}
            ).wait_send()

    def drained(q, _):
        for step in range(n_long):
            long_copy(long_in.at[step, q], step, q).wait_send()
        for step in range(n_short):
            short_copy(short_in.at[step, q], step, q).wait_send()
        return 0

    lax.fori_loop(0, SUBS, drained, 0)


def shards(sizes, head_input, bc_input, conv_x, conv_bc, log_decay, d_skip, gate_z, norm_gain, w_out):
    ny, nx, nc, nz = sizes
    nj = nx * nc
    length, width = head_input.shape
    heads = log_decay.shape[0]
    slab = N // nj
    out_width = w_out.shape[1] // nz
    ts = length // SUBS
    rows = ts + ts // 4
    n_long = nz // 2
    n_short = n_long - 1
    dma = pltpu.SemaphoreType.DMA
    vmem = pltpu.VMEM
    scratch = [
        vmem((length, width), BF16), vmem((length, 2 * N), BF16),
        vmem((K, width), F32), vmem((K, 2 * N), F32), vmem((heads, length), F32),
        pltpu.SMEM((heads,), F32), vmem((length, width), BF16), vmem((1, width), F32),
        vmem(w_out.shape, BF16),
        dma((9,)),
        vmem((16, width), BF16), vmem((16, 2 * N), BF16), dma((2,)), dma((2,)),
        vmem((length + 8, width), F32), vmem((length + 8, 2 * N), F32),
        vmem((length, width), BF16), vmem((length, 2 * N), BF16),
        vmem((heads, 1, length), F32), vmem((length, width), F32), vmem((length, heads * LANES), F32),
        vmem((length, length), F32), vmem((length, width), BF16), vmem((N, width), BF16),
        vmem((nj, 1, width), F32), dma((nj,)), dma((nj,)),
        vmem((ny, 1, width), F32), dma((ny,)), dma((ny,)),
        vmem((nj, slab, width), BF16), dma((nj,)), dma((nj,)), vmem((nj, slab, width), F32),
        vmem((ny, slab, width), BF16), dma((ny,)), dma((ny,)),
        vmem((nj, slab, width), BF16), vmem((N, width), BF16), dma((nj,)), dma((nj,)),
        vmem((length, width), F32), vmem((length, width), F32), vmem((length, width), BF16),
        vmem((length, LANES), F32),
        vmem((nz, 1, length), F32), dma((nz,)), dma((nz,)),
        vmem((nz, SUBS, rows, 2 * LANES), BF16),
        vmem((max(n_long - 1, 1), SUBS, rows, 2 * LANES), BF16),
        vmem((max(n_short - 1, 1), SUBS, rows, 2 * LANES), BF16),
        vmem((n_long, SUBS, rows, 2 * LANES), BF16),
        vmem((max(n_short, 1), SUBS, rows, 2 * LANES), BF16),
        dma((n_long, SUBS)), dma((n_long, SUBS)),
        dma((max(n_short, 1), SUBS)), dma((max(n_short, 1), SUBS)),
        vmem((length, LANES), F32),
    ]
    return pl.pallas_call(
        functools.partial(kernel, sizes),
        out_shape=jax.ShapeDtypeStruct((length, out_width), BF16),
        in_specs=[pl.BlockSpec(memory_space=pl.ANY)] * 9,
        out_specs=pl.BlockSpec(memory_space=pltpu.VMEM),
        scratch_shapes=scratch,
        compiler_params=pltpu.CompilerParams(
            collective_id=0, has_side_effects=True, vmem_limit_bytes=60 * 1024 * 1024
        ),
        name="layer",
    )(
        head_input, bc_input, conv_x, conv_bc, log_decay, d_skip, gate_z,
        norm_gain.reshape(1, width), w_out,
    )


def solution(mesh):
    n_ctx, nz = mesh.devices.shape
    sizes = (8, 4, 2, nz) if n_ctx == 64 else (2, max(n_ctx // 4, 1), 2, nz)
    split = Mesh(mesh.devices.reshape(sizes), ("y", "x", "c", "z"))
    return jax.shard_map(
        functools.partial(shards, sizes),
        mesh=split,
        in_specs=(
            P(CTX, "z"), P(CTX, None), P(None, "z"), P(), P("z", CTX), P("z"), P(CTX, "z"),
            P("z"), P("z", None),
        ),
        out_specs=P(CTX, "z"),
        check_vma=False,
    )
```

time: 232 us -> 67 us (0.29)
  the two profiles are of different devices: /device:TPU:6 before, /device:TPU:48 now
where the time goes in v1:
time: 67 us; the launch traced here: 66.8 us
  Pallas kernels  63.7 us (95%)
  local copies, waits for them, and re-layouts  3.14 us (5%)
    pallas_call x1, Pallas kernels, shards(): pl.pallas_call(functools.partial(kernel, sizes), out_shape=jax.ShapeDtype...  63.7 us
    pallas_call x1, local copies, waits for them, and re-layouts, shards(): pl.pallas_call(functools.partial(kernel, sizes), out_shape=jax.ShapeDtype...  1.88 us

profile of v1, /device:TPU:48, one launch (start us, length us, event | category | flops | bytes accessed | tf_op | source)
XLA Modules:
  0.0 66.8 jit_solution(11565943393597985719)
XLA Ops:
  0.0 1.3 %reshape.3.gain_hbm = f32[1,640]{1,0:T(1,128)} reshape(f32[640]{0:T(1024)} %param.16) | data formatting | bytes 5120 | tf_op jit(solution)/shard_map/reshape | solution.py:567
  1.3 63.7 %layer.1 = bf16[512,320]{1,0:T(8,128)(2,1)} custom-call(bf16[512,640]{1,0:T(8,128)(2,1)} %x_hbm.1, bf16[512,256]{1,0:T(8,128)(2,1)} %bc_hbm.1, f32[4,640]{1,0:T(4,128)} %cx_hbm.1, f32[4,256]{1,0:T(4,128)} %cbc_hbm.1, f32[10,512]{1,0:T(8,128)} %ld_hbm.1, f32[10]{0:T(128)} %d_hbm.1, bf16[512,640]{1,0:T(8,128)(2,1)} %gate_hbm.1, f32[1,640]{1,0:T(1,128)} %reshape.3.gain_hbm, ...), custom_call_target="tpu_custom_call" | custom-call | tf_op jit(solution)/shard_map/layer/pallas_call | solution.py:555
  64.9 1.9 %copy.10 = bf16[512,320]{0,1:T(8,128)(2,1)} copy(bf16[512,320]{1,0:T(8,128)(2,1)} %layer.1) | data formatting | bytes 655360 | tf_op jit(solution)/shard_map/layer/pallas_call | solution.py:555

commit v2 on v1

--- a/solution.py
+++ b/solution.py
@@ -58,17 +58,16 @@
     x_in, bc_in, cx, cbc, ld, d_skip, gate, gain, w,
     load_sem,
     halo_x, halo_bc, halo_send, halo_recv,
-    xf, bcf, xc, bcc, crow, cum, cum2, gram, scaled, state,
+    xc, bcc, crow, cum, cum2, gram, scaled, state,
     decay_row, decay_send, decay_recv,
     total_row, total_send, total_recv,
     row_buf, row_send, row_recv, prefix,
     y_buf, y_send, y_recv,
     c_out, carried, c_send, c_recv,
-    ya, yb, u, sq_part,
+    ya, yb, sq_part,
     sq_buf, sq_send, sq_recv,
-    chunks, long_out, short_out, long_in, short_in,
+    wt, ut, chunks, long_out, short_out, long_in, short_in,
     long_send, long_recv, short_send, short_recv,
-    rstd,
 ):
     ny, nx, nc, nz = sizes
     nj = nx * nc
@@ -115,35 +114,27 @@
     for k in range(1, nj):
         greet(member(lax.rem(j + k, nj)))
 
+    pl.semaphore_wait(barrier, 2 + (ny - 1) + (nz - 1) + (nj - 1))
+    tail = pl.ds(length - 16, 16)
+    halos = [
+        remote(x_hbm.at[tail], halo_x, halo_send.at[0], halo_recv.at[0], after),
+        remote(bc_hbm.at[tail], halo_bc, halo_send.at[1], halo_recv.at[1], after),
+    ]
+
+    @pl.when(flat < ny * nj - 1)
+    def _():
+        for copy in halos:
+            copy.start()
+
     loads[0].wait()
     padded = jnp.concatenate([ld[...], jnp.zeros((16 - heads, length), F32)], axis=0)
     upper = (iota((length, length), 0) <= iota((length, length), 1)).astype(BF16)
     three = dot(jnp.concatenate(split_three(padded), axis=0), upper, ((1,), (0,)))
     rows = three[0:16] + (three[16:32] + three[32:48])
-    for h in range(heads):
-        crow[h] = rows[h : h + 1]
     stacked = jnp.concatenate(split_three(rows), axis=0)
     pick = (iota((48, width), 0) & 15) == lax.shift_right_logical(iota((48, width), 1), 6)
     cum[...] = dot(stacked, pick.astype(BF16), ((0,), (0,)))
-    wide = heads * LANES
-    pick2 = (iota((48, wide), 0) & 15) == lax.shift_right_logical(iota((48, wide), 1), 7)
-    cum2[...] = dot(stacked, pick2.astype(BF16), ((0,), (0,)))
     decay_row[j] = cum[length - 1 : length, :]
-
-    loads[1].wait()
-    loads[2].wait()
-    pl.semaphore_wait(barrier, 2 + (ny - 1) + (nz - 1) + (nj - 1))
-
-    tail = pl.ds(length - 16, 16)
-    halos = [
-        remote(x_in.at[tail], halo_x, halo_send.at[0], halo_recv.at[0], after),
-        remote(bc_in.at[tail], halo_bc, halo_send.at[1], halo_recv.at[1], after),
-    ]
-
-    @pl.when(flat < ny * nj - 1)
-    def _():
-        for copy in halos:
-            copy.start()
 
     decays = []
     for k in range(1, nj):
@@ -154,48 +145,48 @@
         copy.start()
         decays.append(copy)
 
-    loads[3].wait()
-    loads[4].wait()
-    xf[0:8, :] = jnp.zeros((8, width), F32)
-    bcf[0:8, :] = jnp.zeros((8, 2 * N), F32)
-
-    def widen(i, _):
-        r = pl.multiple_of(i * ROWS, ROWS)
-        xf[pl.ds(r + 8, ROWS), :] = x_in[pl.ds(r, ROWS), :].astype(F32)
-        bcf[pl.ds(r + 8, ROWS), :] = bc_in[pl.ds(r, ROWS), :].astype(F32)
-        return 0
-
-    lax.fori_loop(0, length // ROWS, widen, 0)
-
-    def filtered(source, taps, r):
-        block = source[pl.ds(r, ROWS + 8), :]
-        total = taps[K - 1 : K, :] * block[8:]
+    for load in loads[1:5]:
+        load.wait()
+
+    def filtered(block, taps):
+        total = taps[K - 1 : K, :] * block[16:]
         for tap in range(K - 1):
-            total = total + taps[tap : tap + 1, :] * pltpu.roll(block, K - 1 - tap, 0)[8:]
+            total = total + taps[tap : tap + 1, :] * pltpu.roll(block, K - 1 - tap, 0)[16:]
         return silu(total).astype(BF16)
 
-    def convolve(i, _):
-        r = pl.multiple_of(i * ROWS, ROWS)
-        here = pl.ds(r, ROWS)
-        conv = filtered(xf, cx, r)
+    def convolve(here, block_x, block_bc):
+        conv = filtered(block_x.astype(F32), cx)
         xc[here, :] = conv
-        bcc[here, :] = filtered(bcf, cbc, r)
+        bcc[here, :] = filtered(block_bc.astype(F32), cbc)
         weight = jnp.exp(cum[length - 1 : length, :] - cum[here, :])
         scaled[here, :] = (conv.astype(F32) * weight).astype(BF16)
-        return 0
-
-    lax.fori_loop(1, length // ROWS, convolve, 0)
+
+    def convolve_at(i, _):
+        r = pl.multiple_of(i * ROWS, ROWS)
+        block = pl.ds(pl.multiple_of(r - 16, 16), ROWS + 16)
+        convolve(pl.ds(r, ROWS), x_in[block, :], bc_in[block, :])
+        return 0
+
+    lax.fori_loop(1, length // ROWS, convolve_at, 0)
+    later = dot(bcc[ROWS:length, 0:N], scaled[ROWS:length, :], ((0,), (0,)))
+
+    @pl.when(flat == 0)
+    def _():
+        halo_x[...] = jnp.zeros((16, width), BF16)
+        halo_bc[...] = jnp.zeros((16, 2 * N), BF16)
 
     @pl.when(flat > 0)
     def _():
         for copy in halos:
             copy.wait_recv()
-        xf[0:8, :] = halo_x[8:16, :].astype(F32)
-        bcf[0:8, :] = halo_bc[8:16, :].astype(F32)
-
-    convolve(0, 0)
-
-    state[...] = dot(bcc[:, 0:N], scaled[...], ((0,), (0,))).astype(BF16)
+
+    convolve(
+        slice(0, ROWS),
+        jnp.concatenate([halo_x[...], x_in[0:ROWS, :]], axis=0),
+        jnp.concatenate([halo_bc[...], bc_in[0:ROWS, :]], axis=0),
+    )
+
+    state[...] = (later + dot(bcc[0:ROWS, 0:N], scaled[0:ROWS, :], ((0,), (0,)))).astype(BF16)
     row_buf[j] = state[pl.ds(pl.multiple_of(j * slab, slab), slab), :]
     sent = []
     for k in range(1, nj):
@@ -229,6 +220,11 @@
         copy.start()
         totals.append(copy)
 
+    for h in range(heads):
+        crow[h] = rows[h : h + 1]
+    wide = heads * LANES
+    pick2 = (iota((48, wide), 0) & 15) == lax.shift_right_logical(iota((48, wide), 1), 7)
+    cum2[...] = dot(stacked, pick2.astype(BF16), ((0,), (0,)))
     gram[...] = dot(bcc[:, N : 2 * N], bcc[:, 0:N], ((1,), (1,)))
     left = iota((LANES, LANES), 1) < 64
     causal = iota((LANES, LANES), 0) >= iota((LANES, LANES), 1)
@@ -290,6 +286,16 @@
 
     lax.fori_loop(0, length // ROWS, gates, 0)
 
+    loads[8].wait()
+
+    def turn(i, _):
+        here = pl.ds(pl.multiple_of(i * LANES, LANES), LANES)
+        wt[here, :] = w[:, here].T
+        return 0
+
+    blocks = w.shape[1] // LANES
+    lax.fori_loop(0, blocks * 5 // 8, turn, 0)
+
     for k in range(1, ny):
         other = lax.rem(y + k, ny)
         remote(
@@ -322,7 +328,8 @@
         copy.start()
         returned.append(copy)
     loads[7].wait()
-    loads[8].wait()
+    lax.fori_loop(blocks * 5 // 8, blocks, turn, 0)
+    amount = gain[...].reshape(1, width)
     for k in range(1, nj):
         other = lax.rem(j + k, nj)
         theirs = carried.at[pl.ds(pl.multiple_of(other * slab, slab), slab)]
@@ -332,7 +339,7 @@
         here = pl.ds(pl.multiple_of(i * LANES, LANES), LANES)
         from_state = dot(bcc[here, N : 2 * N], carried[...], ((1,), (0,)))
         gated = ya[here, :] + yb[here, :] * from_state
-        u[here, :] = (gated * gain[...]).astype(BF16)
+        ut[:, here] = (gated * amount).astype(BF16).T
         square = gated * gated
         total = square[:, 0:LANES]
         for part in range(1, pairs):
@@ -342,25 +349,14 @@
 
     lax.fori_loop(0, length // LANES, finish, 0)
 
-    ts = length // SUBS
-    quarter = ts // 4
-    half = iota((quarter, LANES), 1) < 64
-
-    def project(p):
-        col = pl.multiple_of(p * 5 * LANES, LANES)
-        for begin, dest in ((0, 2 * p), (3 * LANES, 2 * p + 1)):
-            part = dot(u[...], w[:, pl.ds(col + begin, 2 * LANES)], ((1,), (0,)))
-            for q in range(SUBS):
-                chunks[dest, q, 0:ts, :] = part[q * ts : (q + 1) * ts].astype(BF16)
-        middle = dot(u[...], w[:, pl.ds(col + 2 * LANES, LANES)], ((1,), (0,)))
-        turned = pltpu.roll(middle, 64, 1)
+    rows_out = out_ref.shape[0]
+    piece = rows_out // SUBS
+
+    def project(d):
+        here = pl.ds(pl.multiple_of(d * rows_out, 64), rows_out)
+        part = dot(wt[here, :], ut[...], ((1,), (0,))).astype(BF16)
         for q in range(SUBS):
-            m = [middle[q * ts + g * quarter : q * ts + (g + 1) * quarter] for g in range(4)]
-            r = [turned[q * ts + g * quarter : q * ts + (g + 1) * quarter] for g in range(4)]
-            even = [jnp.where(half, m[g], r[g + 1]) for g in (0, 2)]
-            odd = [jnp.where(half, r[g], m[g + 1]) for g in (0, 2)]
-            chunks[2 * p, q, ts : ts + quarter, :] = jnp.concatenate(even, axis=1).astype(BF16)
-            chunks[2 * p + 1, q, ts : ts + quarter, :] = jnp.concatenate(odd, axis=1).astype(BF16)
+            chunks[d, q] = part[q * piece : (q + 1) * piece]
 
     sign = 1 - 2 * c
     n_long = nz // 2
@@ -381,12 +377,6 @@
             {"z": towards(-1)},
         )
 
-    half_nz = nz // 2
-    first = lax.div(towards(n_long), 2)
-
-    def pair_at(offset):
-        return lax.rem(first + offset * sign + 2 * half_nz, half_nz)
-
     def start_long(q, _):
         long_copy(chunks.at[towards(n_long), q], 0, q).start()
         return 0
@@ -395,17 +385,15 @@
         short_copy(chunks.at[towards(-n_short), q], 0, q).start()
         return 0
 
-    order = [0, 1, -1, 2][:half_nz] if half_nz > 2 else list(range(half_nz))
-    project(pair_at(order[0]))
+    project(towards(n_long))
     lax.fori_loop(0, SUBS, start_long, 0)
-    if half_nz > 1:
-        project(pair_at(order[1]))
     if n_short:
+        project(towards(-n_short))
         lax.fori_loop(0, SUBS, start_short, 0)
 
     squares = jnp.zeros((16, length), F32)
-    for piece in split_three(sq_part[...]):
-        squares = squares + dot(jnp.ones((16, LANES), BF16), piece, ((1,), (1,)))
+    for term in split_three(sq_part[...]):
+        squares = squares + dot(jnp.ones((16, LANES), BF16), term, ((1,), (1,)))
     sq_buf[z] = squares[0:1, :]
     shared = []
     for k in range(1, nz):
@@ -414,8 +402,12 @@
         )
         copy.start()
         shared.append(copy)
-    for offset in order[2:]:
-        project(pair_at(offset))
+
+    for step in range(1, n_long):
+        project(towards(n_long - step))
+        if step < n_short:
+            project(towards(step - n_short))
+    project(z)
 
     for step in range(1, n_long):
 
@@ -442,15 +434,7 @@
     summed = sq_buf[0]
     for i in range(1, nz):
         summed = summed + sq_buf[i]
-    high, middle, low = split_three(summed)
-    which = iota((16, length), 0)
-    table = jnp.where(
-        which == 0,
-        high.astype(F32),
-        jnp.where(which == 1, middle.astype(F32), jnp.where(which == 2, low.astype(F32), 0.0)),
-    ).astype(BF16)
-    spread = dot(table, jnp.ones((16, LANES), BF16), ((0,), (0,)))
-    rstd[...] = lax.rsqrt(spread * (1.0 / (width * nz)) + 1e-5)
+    scale = lax.rsqrt(summed * (1.0 / (width * nz)) + 1e-5)
 
     def deliver(q, _):
         long_copy(long_in.at[n_long - 1, q], n_long - 1, q).wait_recv()
@@ -458,30 +442,7 @@
         if n_short:
             short_copy(short_in.at[n_short - 1, q], n_short - 1, q).wait_recv()
             total = total + short_in[n_short - 1, q].astype(F32)
-        base = pl.multiple_of(q * ts, ts)
-        here = pl.ds(base, ts)
-        scale = rstd[here, :]
-        a0 = total[0:ts, 0:LANES] * scale
-        a1 = total[0:ts, LANES : 2 * LANES] * scale
-        b0 = total[ts : ts + quarter, 0:LANES]
-        b1 = total[ts : ts + quarter, LANES : 2 * LANES]
-        b = jnp.concatenate([b0, pltpu.roll(b0, 64, 1), b1, pltpu.roll(b1, 64, 1)], axis=0) * scale
-
-        @pl.when(lax.rem(z, 2) == 0)
-        def _():
-            out_ref[here, 0:LANES] = a0.astype(BF16)
-            out_ref[here, LANES : 2 * LANES] = a1.astype(BF16)
-            out_ref[here, 2 * LANES : 2 * LANES + 64] = b[:, 0:64].astype(BF16)
-
-        @pl.when(lax.rem(z, 2) == 1)
-        def _():
-            r0 = pltpu.roll(a0, 64, 1)
-            r1 = pltpu.roll(a1, 64, 1)
-            low_half = iota((ts, LANES), 1) < 64
-            out_ref[here, 0:LANES] = jnp.where(low_half, b, r0).astype(BF16)
-            out_ref[here, LANES : 2 * LANES] = jnp.where(low_half, r0, r1).astype(BF16)
-            out_ref[here, 2 * LANES : 2 * LANES + 64] = r1[:, 0:64].astype(BF16)
-
+        out_ref[pl.ds(pl.multiple_of(q * piece, piece), piece), :] = (total * scale).astype(BF16)
         return 0
 
     lax.fori_loop(0, SUBS, deliver, 0)
@@ -518,8 +479,7 @@
     heads = log_decay.shape[0]
     slab = N // nj
     out_width = w_out.shape[1] // nz
-    ts = length // SUBS
-    rows = ts + ts // 4
+    piece = out_width // SUBS
     n_long = nz // 2
     n_short = n_long - 1
     dma = pltpu.SemaphoreType.DMA
@@ -527,11 +487,10 @@
     scratch = [
         vmem((length, width), BF16), vmem((length, 2 * N), BF16),
         vmem((K, width), F32), vmem((K, 2 * N), F32), vmem((heads, length), F32),
-        pltpu.SMEM((heads,), F32), vmem((length, width), BF16), vmem((1, width), F32),
+        pltpu.SMEM((heads,), F32), vmem((length, width), BF16), vmem((width,), F32),
         vmem(w_out.shape, BF16),
         dma((9,)),
         vmem((16, width), BF16), vmem((16, 2 * N), BF16), dma((2,)), dma((2,)),
-        vmem((length + 8, width), F32), vmem((length + 8, 2 * N), F32),
         vmem((length, width), BF16), vmem((length, 2 * N), BF16),
         vmem((heads, 1, length), F32), vmem((length, width), F32), vmem((length, heads * LANES), F32),
         vmem((length, length), F32), vmem((length, width), BF16), vmem((N, width), BF16),
@@ -540,21 +499,20 @@
         vmem((nj, slab, width), BF16), dma((nj,)), dma((nj,)), vmem((nj, slab, width), F32),
         vmem((ny, slab, width), BF16), dma((ny,)), dma((ny,)),
         vmem((nj, slab, width), BF16), vmem((N, width), BF16), dma((nj,)), dma((nj,)),
-        vmem((length, width), F32), vmem((length, width), F32), vmem((length, width), BF16),
-        vmem((length, LANES), F32),
+        vmem((length, width), F32), vmem((length, width), F32), vmem((length, LANES), F32),
         vmem((nz, 1, length), F32), dma((nz,)), dma((nz,)),
-        vmem((nz, SUBS, rows, 2 * LANES), BF16),
-        vmem((max(n_long - 1, 1), SUBS, rows, 2 * LANES), BF16),
-        vmem((max(n_short - 1, 1), SUBS, rows, 2 * LANES), BF16),
-        vmem((n_long, SUBS, rows, 2 * LANES), BF16),
-        vmem((max(n_short, 1), SUBS, rows, 2 * LANES), BF16),
+        vmem(w_out.shape[::-1], BF16), vmem((width, length), BF16),
+        vmem((nz, SUBS, piece, length), BF16),
+        vmem((max(n_long - 1, 1), SUBS, piece, length), BF16),
+        vmem((max(n_short - 1, 1), SUBS, piece, length), BF16),
+        vmem((n_long, SUBS, piece, length), BF16),
+        vmem((max(n_short, 1), SUBS, piece, length), BF16),
         dma((n_long, SUBS)), dma((n_long, SUBS)),
         dma((max(n_short, 1), SUBS)), dma((max(n_short, 1), SUBS)),
-        vmem((length, LANES), F32),
     ]
     return pl.pallas_call(
         functools.partial(kernel, sizes),
-        out_shape=jax.ShapeDtypeStruct((length, out_width), BF16),
+        out_shape=jax.ShapeDtypeStruct((out_width, length), BF16),
         in_specs=[pl.BlockSpec(memory_space=pl.ANY)] * 9,
         out_specs=pl.BlockSpec(memory_space=pltpu.VMEM),
         scratch_shapes=scratch,
@@ -564,8 +522,8 @@
         name="layer",
     )(
         head_input, bc_input, conv_x, conv_bc, log_decay, d_skip, gate_z,
-        norm_gain.reshape(1, width), w_out,
-    )
+        norm_gain, w_out,
+    ).T
 
 
 def solution(mesh):

time: 67 us -> 65.5 us (0.978)
  local copies, waits for them, and re-layouts: 3.14 us -> 1.72 us
    pallas_call x1 -> x0, local copies, waits for them, and re-layouts: 1.88 us -> none  [shards(): pl.pallas_call(functools.partial(kernel, sizes), out_shape=jax.ShapeDtype...]
    unnamed x0 -> x1, local copies, waits for them, and re-layouts: none -> 1.72 us
    reshape x1 -> x0, local copies, waits for them, and re-layouts: 1.27 us -> none  [shards(): norm_gain.reshape(1, width)]
where the time goes in v2:
time: 65.5 us; the launch traced here: 65.4 us
  Pallas kernels  63.6 us (97%)
  local copies, waits for them, and re-layouts  1.72 us (3%)
    pallas_call x1, Pallas kernels, shards(): pl.pallas_call(functools.partial(kernel, sizes), out_shape=jax.ShapeDtype...  63.6 us
    unnamed x1, local copies, waits for them, and re-layouts  1.72 us

profile of v2, /device:TPU:48, one launch (start us, length us, event | category | flops | bytes accessed | tf_op | source)
XLA Modules:
  0.0 65.4 jit_solution(17625828550439352454)
XLA Ops:
  0.0 63.6 %layer.1 = bf16[320,512]{1,0:T(8,128)(2,1)} custom-call(bf16[512,640]{1,0:T(8,128)(2,1)} %x_hbm.1, bf16[512,256]{1,0:T(8,128)(2,1)} %bc_hbm.1, f32[4,640]{1,0:T(4,128)} %cx_hbm.1, f32[4,256]{1,0:T(4,128)} %cbc_hbm.1, f32[10,512]{1,0:T(8,128)} %ld_hbm.1, f32[10]{0:T(128)} %d_hbm.1, bf16[512,640]{1,0:T(8,128)(2,1)} %gate_hbm.1, f32[640]{0:T(1024)} %gain_hbm.1, ...), custom_call_target="tpu_custom_call" | custom-call | tf_op jit(solution)/shard_map/layer/pallas_call | solution.py:513
  63.6 1.7 %copy.11 = bf16[512,320]{0,1:T(8,128)(2,1)} copy(bf16[512,320]{0,1:T(8,128)(2,1)} %bitcast.1) | data formatting | bytes 655360

commit v3 on v2

--- a/solution.py
+++ b/solution.py
@@ -28,8 +28,8 @@
 
 
 def silu(value):
-    small = jnp.exp(-jnp.abs(value))
-    return value * jnp.where(value >= 0, 1.0, small) / (1.0 + small)
+    half = 0.5 * value
+    return half + half * jnp.tanh(half)
 
 
 def dot(a, b, dims):
@@ -58,7 +58,7 @@
     x_in, bc_in, cx, cbc, ld, d_skip, gate, gain, w,
     load_sem,
     halo_x, halo_bc, halo_send, halo_recv,
-    xc, bcc, crow, cum, cum2, gram, scaled, state,
+    xc, bcc, crow, cum, cum2, gram, scaled, later, state,
     decay_row, decay_send, decay_recv,
     total_row, total_send, total_recv,
     row_buf, row_send, row_recv, prefix,
@@ -78,6 +78,10 @@
     heads, length = ld.shape
     width = x_in.shape[1]
     pairs = width // LANES
+    cut = (pairs + 1) // 2 * LANES
+    halves = [slice(0, cut), slice(cut, width)]
+    row_steps = sorted(range(1, nj), key=lambda k: -min(k, nj - k))
+    y_steps = sorted(range(1, ny), key=lambda k: -min(k, ny - k))
 
     loads = [
         pltpu.make_async_copy(source, target, load_sem.at[i])
@@ -168,7 +172,7 @@
         return 0
 
     lax.fori_loop(1, length // ROWS, convolve_at, 0)
-    later = dot(bcc[ROWS:length, 0:N], scaled[ROWS:length, :], ((0,), (0,)))
+    later[...] = dot(bcc[ROWS:length, 0:N], scaled[ROWS:length, :], ((0,), (0,)))
 
     @pl.when(flat == 0)
     def _():
@@ -186,20 +190,25 @@
         jnp.concatenate([halo_bc[...], bc_in[0:ROWS, :]], axis=0),
     )
 
-    state[...] = (later + dot(bcc[0:ROWS, 0:N], scaled[0:ROWS, :], ((0,), (0,)))).astype(BF16)
-    row_buf[j] = state[pl.ds(pl.multiple_of(j * slab, slab), slab), :]
+    def slice_of(index):
+        return pl.ds(pl.multiple_of(index * slab, slab), slab)
+
     sent = []
-    for k in range(1, nj):
-        other = lax.rem(j + k, nj)
-        copy = remote(
-            state.at[pl.ds(pl.multiple_of(other * slab, slab), slab)],
-            row_buf.at[j],
-            row_send.at[k],
-            row_recv.at[j],
-            member(other),
-        )
-        copy.start()
-        sent.append(copy)
+    for half, lanes in enumerate(halves):
+        first = dot(bcc[0:ROWS, 0:N], scaled[0:ROWS, lanes], ((0,), (0,)))
+        state[:, lanes] = (later[:, lanes] + first).astype(BF16)
+        for k in row_steps:
+            other = lax.rem(j + k, nj)
+            copy = remote(
+                state.at[slice_of(other), lanes],
+                row_buf.at[j, :, lanes],
+                row_send.at[half, k],
+                row_recv.at[half, j],
+                member(other),
+            )
+            copy.start()
+            sent.append(copy)
+        row_buf[j, :, lanes] = state[slice_of(j), lanes]
 
     for k in range(1, nj):
         other = lax.rem(j + k, nj)
@@ -255,23 +264,31 @@
 
     lax.fori_loop(0, 2, local_pair, 0)
 
-    for k in range(1, nj):
-        other = lax.rem(j + k, nj)
-        remote(
-            row_buf.at[other], row_buf.at[other], row_send.at[k], row_recv.at[other], member(other)
-        ).wait_recv()
-    running = jnp.zeros((slab, width), F32)
-    for i in range(nj):
-        prefix[i] = running
-        running = jnp.exp(decay_row[i]) * running + row_buf[i].astype(F32)
-    y_buf[y] = running.astype(BF16)
-    for k in range(1, ny):
-
-        @pl.when(y + k < ny)
-        def _(k=k):
+    def y_copy(half, k):
+        lanes = halves[half]
+        return remote(
+            y_buf.at[y, :, lanes], y_buf.at[y, :, lanes], y_send.at[half, k], y_recv.at[half, y],
+            {"y": lax.rem(y + k, ny)},
+        )
+
+    for half, lanes in enumerate(halves):
+        for k in row_steps:
+            other = lax.rem(j + k, nj)
+            theirs = row_buf.at[other, :, lanes]
             remote(
-                y_buf.at[y], y_buf.at[y], y_send.at[k], y_recv.at[y], {"y": lax.rem(y + k, ny)}
-            ).start()
+                theirs, theirs, row_send.at[half, k], row_recv.at[half, other], member(other)
+            ).wait_recv()
+        running = jnp.zeros((slab, lanes.stop - lanes.start), F32)
+        for i in range(nj):
+            prefix[i, :, lanes] = running
+            running = jnp.exp(decay_row[i, :, lanes]) * running
+            running = running + row_buf[i, :, lanes].astype(F32)
+        y_buf[y, :, lanes] = running.astype(BF16)
+        for k in y_steps:
+
+            @pl.when(y + k < ny)
+            def _(half=half, k=k):
+                y_copy(half, k).start()
 
     lax.fori_loop(2, pairs, local_pair, 0)
 
@@ -302,61 +319,82 @@
             total_row.at[other], total_row.at[other], total_send.at[k], total_recv.at[other],
             {"y": other},
         ).wait_recv()
-    for k in range(1, ny):
-
-        @pl.when(y >= k)
-        def _(k=k):
-            other = lax.rem(y - k + ny, ny)
-            remote(
-                y_buf.at[other], y_buf.at[other], y_send.at[k], y_recv.at[other], {"y": other}
-            ).wait_recv()
-
-    def earlier(i, total):
-        return jnp.exp(total_row[i]) * total + y_buf[i].astype(F32)
-
-    base = lax.fori_loop(0, y, earlier, jnp.zeros((slab, width), F32))
-    fade = jnp.zeros((1, width), F32)
-    for i in range(nj):
-        c_out[i] = (jnp.exp(fade) * base + prefix[i]).astype(BF16)
-        fade = fade + decay_row[i]
-    mine = pl.ds(pl.multiple_of(j * slab, slab), slab)
-    carried[mine, :] = c_out[j]
     returned = []
-    for k in range(1, nj):
-        other = lax.rem(j + k, nj)
-        copy = remote(c_out.at[other], carried.at[mine], c_send.at[k], c_recv.at[j], member(other))
-        copy.start()
-        returned.append(copy)
+    for half, lanes in enumerate(halves):
+        for k in y_steps:
+
+            @pl.when(y >= k)
+            def _(half=half, lanes=lanes, k=k):
+                other = lax.rem(y - k + ny, ny)
+                theirs = y_buf.at[other, :, lanes]
+                remote(
+                    theirs, theirs, y_send.at[half, k], y_recv.at[half, other], {"y": other}
+                ).wait_recv()
+
+        def earlier(i, total, lanes=lanes):
+            return jnp.exp(total_row[i, :, lanes]) * total + y_buf[i, :, lanes].astype(F32)
+
+        part_width = lanes.stop - lanes.start
+        base = lax.fori_loop(0, y, earlier, jnp.zeros((slab, part_width), F32))
+        fade = jnp.zeros((1, part_width), F32)
+        for i in range(nj):
+            c_out[i, :, lanes] = (jnp.exp(fade) * base + prefix[i, :, lanes]).astype(BF16)
+            fade = fade + decay_row[i, :, lanes]
+        for k in row_steps:
+            other = lax.rem(j + k, nj)
+            copy = remote(
+                c_out.at[other, :, lanes], carried.at[slice_of(j), lanes], c_send.at[half, k],
+                c_recv.at[half, j], member(other),
+            )
+            copy.start()
+            returned.append(copy)
+        carried[slice_of(j), lanes] = c_out[j, :, lanes]
+
     loads[7].wait()
     lax.fori_loop(blocks * 5 // 8, blocks, turn, 0)
     amount = gain[...].reshape(1, width)
-    for k in range(1, nj):
-        other = lax.rem(j + k, nj)
-        theirs = carried.at[pl.ds(pl.multiple_of(other * slab, slab), slab)]
-        remote(theirs, theirs, c_send.at[k], c_recv.at[other], member(other)).wait_recv()
-
-    def finish(i, _):
-        here = pl.ds(pl.multiple_of(i * LANES, LANES), LANES)
-        from_state = dot(bcc[here, N : 2 * N], carried[...], ((1,), (0,)))
-        gated = ya[here, :] + yb[here, :] * from_state
-        ut[:, here] = (gated * amount).astype(BF16).T
+
+    def await_carried(half):
+        for k in row_steps:
+            other = lax.rem(j + k, nj)
+            theirs = carried.at[slice_of(other), halves[half]]
+            remote(
+                theirs, theirs, c_send.at[half, k], c_recv.at[half, other], member(other)
+            ).wait_recv()
+
+    def finish(half, here):
+        lanes = halves[half]
+        from_state = dot(bcc[here, N : 2 * N], carried[:, lanes], ((1,), (0,)))
+        gated = ya[here, lanes] + yb[here, lanes] * from_state
+        ut[lanes, here] = (gated * amount[:, lanes]).astype(BF16).T
         square = gated * gated
         total = square[:, 0:LANES]
-        for part in range(1, pairs):
-            total = total + square[:, part * LANES : (part + 1) * LANES]
-        sq_part[here, :] = total
-        return 0
-
-    lax.fori_loop(0, length // LANES, finish, 0)
+        for begin in range(LANES, lanes.stop - lanes.start, LANES):
+            total = total + square[:, begin : begin + LANES]
+        sq_part[here, :] = total if half == 0 else sq_part[here, :] + total
+
+    def finish_first(i, _):
+        finish(0, pl.ds(pl.multiple_of(i * LANES, LANES), LANES))
+        return 0
+
+    await_carried(0)
+    lax.fori_loop(0, length // LANES, finish_first, 0)
 
     rows_out = out_ref.shape[0]
-    piece = rows_out // SUBS
+    piece = length // SUBS
+
+    def tokens(q):
+        return pl.ds(pl.multiple_of(q * piece, piece), piece)
+
+    def project_piece(d, q):
+        here = pl.ds(pl.multiple_of(d * rows_out, 64), rows_out)
+        chunks[d, q] = dot(wt[here, :], ut[:, tokens(q)], ((1,), (0,))).astype(BF16)
 
     def project(d):
         here = pl.ds(pl.multiple_of(d * rows_out, 64), rows_out)
         part = dot(wt[here, :], ut[...], ((1,), (0,))).astype(BF16)
         for q in range(SUBS):
-            chunks[d, q] = part[q * piece : (q + 1) * piece]
+            chunks[d, q] = part[:, q * piece : (q + 1) * piece]
 
     sign = 1 - 2 * c
     n_long = nz // 2
@@ -377,19 +415,17 @@
             {"z": towards(-1)},
         )
 
-    def start_long(q, _):
+    def begin(q, _):
+        finish(1, tokens(q))
+        project_piece(towards(n_long), q)
         long_copy(chunks.at[towards(n_long), q], 0, q).start()
-        return 0
-
-    def start_short(q, _):
-        short_copy(chunks.at[towards(-n_short), q], 0, q).start()
-        return 0
-
-    project(towards(n_long))
-    lax.fori_loop(0, SUBS, start_long, 0)
-    if n_short:
-        project(towards(-n_short))
-        lax.fori_loop(0, SUBS, start_short, 0)
+        if n_short:
+            project_piece(towards(-n_short), q)
+            short_copy(chunks.at[towards(-n_short), q], 0, q).start()
+        return 0
+
+    await_carried(1)
+    lax.fori_loop(0, SUBS, begin, 0)
 
     squares = jnp.zeros((16, length), F32)
     for term in split_three(sq_part[...]):
@@ -431,18 +467,17 @@
     for k in range(1, nz):
         other = lax.rem(z + k, nz)
         remote(sq_buf.at[other], sq_buf.at[other], sq_send.at[k], sq_recv.at[other], {"z": other}).wait_recv()
-    summed = sq_buf[0]
-    for i in range(1, nz):
-        summed = summed + sq_buf[i]
-    scale = lax.rsqrt(summed * (1.0 / (width * nz)) + 1e-5)
-
     def deliver(q, _):
         long_copy(long_in.at[n_long - 1, q], n_long - 1, q).wait_recv()
         total = chunks[z, q].astype(F32) + long_in[n_long - 1, q].astype(F32)
         if n_short:
             short_copy(short_in.at[n_short - 1, q], n_short - 1, q).wait_recv()
             total = total + short_in[n_short - 1, q].astype(F32)
-        out_ref[pl.ds(pl.multiple_of(q * piece, piece), piece), :] = (total * scale).astype(BF16)
+        summed = sq_buf[0, :, tokens(q)]
+        for i in range(1, nz):
+            summed = summed + sq_buf[i, :, tokens(q)]
+        scale = lax.rsqrt(summed * (1.0 / (width * nz)) + 1e-5)
+        out_ref[:, tokens(q)] = (total * scale).astype(BF16)
         return 0
 
     lax.fori_loop(0, SUBS, deliver, 0)
@@ -454,13 +489,12 @@
 
     for copy in decays + totals + sent + returned + shared:
         copy.wait_send()
-    for k in range(1, ny):
-
-        @pl.when(y + k < ny)
-        def _(k=k):
-            remote(
-                y_buf.at[y], y_buf.at[y], y_send.at[k], y_recv.at[y], {"y": lax.rem(y + k, ny)}
-            ).wait_send()
+    for half in range(2):
+        for k in y_steps:
+
+            @pl.when(y + k < ny)
+            def _(half=half, k=k):
+                y_copy(half, k).wait_send()
 
     def drained(q, _):
         for step in range(n_long):
@@ -479,7 +513,7 @@
     heads = log_decay.shape[0]
     slab = N // nj
     out_width = w_out.shape[1] // nz
-    piece = out_width // SUBS
+    piece = length // SUBS
     n_long = nz // 2
     n_short = n_long - 1
     dma = pltpu.SemaphoreType.DMA
@@ -493,20 +527,21 @@
         vmem((16, width), BF16), vmem((16, 2 * N), BF16), dma((2,)), dma((2,)),
         vmem((length, width), BF16), vmem((length, 2 * N), BF16),
         vmem((heads, 1, length), F32), vmem((length, width), F32), vmem((length, heads * LANES), F32),
-        vmem((length, length), F32), vmem((length, width), BF16), vmem((N, width), BF16),
+        vmem((length, length), F32), vmem((length, width), BF16),
+        vmem((N, width), F32), vmem((N, width), BF16),
         vmem((nj, 1, width), F32), dma((nj,)), dma((nj,)),
         vmem((ny, 1, width), F32), dma((ny,)), dma((ny,)),
-        vmem((nj, slab, width), BF16), dma((nj,)), dma((nj,)), vmem((nj, slab, width), F32),
-        vmem((ny, slab, width), BF16), dma((ny,)), dma((ny,)),
-        vmem((nj, slab, width), BF16), vmem((N, width), BF16), dma((nj,)), dma((nj,)),
+        vmem((nj, slab, width), BF16), dma((2, nj)), dma((2, nj)), vmem((nj, slab, width), F32),
+        vmem((ny, slab, width), BF16), dma((2, ny)), dma((2, ny)),
+        vmem((nj, slab, width), BF16), vmem((N, width), BF16), dma((2, nj)), dma((2, nj)),
         vmem((length, width), F32), vmem((length, width), F32), vmem((length, LANES), F32),
         vmem((nz, 1, length), F32), dma((nz,)), dma((nz,)),
         vmem(w_out.shape[::-1], BF16), vmem((width, length), BF16),
-        vmem((nz, SUBS, piece, length), BF16),
-        vmem((max(n_long - 1, 1), SUBS, piece, length), BF16),
-        vmem((max(n_short - 1, 1), SUBS, piece, length), BF16),
-        vmem((n_long, SUBS, piece, length), BF16),
-        vmem((max(n_short, 1), SUBS, piece, length), BF16),
+        vmem((nz, SUBS, out_width, piece), BF16),
+        vmem((max(n_long - 1, 1), SUBS, out_width, piece), BF16),
+        vmem((max(n_short - 1, 1), SUBS, out_width, piece), BF16),
+        vmem((n_long, SUBS, out_width, piece), BF16),
+        vmem((max(n_short, 1), SUBS, out_width, piece), BF16),
         dma((n_long, SUBS)), dma((n_long, SUBS)),
         dma((max(n_short, 1), SUBS)), dma((max(n_short, 1), SUBS)),
     ]

time: 65.5 us -> 63.4 us (0.968)
  Pallas kernels: 63.6 us -> 61.5 us
    pallas_call x1, Pallas kernels: 63.6 us -> 61.5 us  [shards(): pl.pallas_call(functools.partial(kernel, sizes), out_shape=jax.ShapeDtype...]
where the time goes in v3:
time: 63.4 us; the launch traced here: 63.2 us
  Pallas kernels  61.5 us (97%)
  local copies, waits for them, and re-layouts  1.72 us (3%)
    pallas_call x1, Pallas kernels, shards(): pl.pallas_call(functools.partial(kernel, sizes), out_shape=jax.ShapeDtype...  61.5 us
    unnamed x1, local copies, waits for them, and re-layouts  1.72 us

profile of v3, /device:TPU:48, one launch (start us, length us, event | category | flops | bytes accessed | tf_op | source)
XLA Modules:
  0.0 63.2 jit_solution(7980246104047512982)
XLA Ops:
  0.0 61.5 %layer.1 = bf16[320,512]{1,0:T(8,128)(2,1)} custom-call(bf16[512,640]{1,0:T(8,128)(2,1)} %x_hbm.1, bf16[512,256]{1,0:T(8,128)(2,1)} %bc_hbm.1, f32[4,640]{1,0:T(4,128)} %cx_hbm.1, f32[4,256]{1,0:T(4,128)} %cbc_hbm.1, f32[10,512]{1,0:T(8,128)} %ld_hbm.1, f32[10]{0:T(128)} %d_hbm.1, bf16[512,640]{1,0:T(8,128)(2,1)} %gate_hbm.1, f32[640]{0:T(1024)} %gain_hbm.1, ...), custom_call_target="tpu_custom_call" | custom-call | tf_op jit(solution)/shard_map/layer/pallas_call | solution.py:548
  61.5 1.7 %copy.11 = bf16[512,320]{0,1:T(8,128)(2,1)} copy(bf16[512,320]{0,1:T(8,128)(2,1)} %bitcast.1) | data formatting | bytes 655360

commit v4 on v3

--- a/solution.py
+++ b/solution.py
@@ -547,7 +547,7 @@
     ]
     return pl.pallas_call(
         functools.partial(kernel, sizes),
-        out_shape=jax.ShapeDtypeStruct((out_width, length), BF16),
+        out_shape=pltpu.VMEM((out_width, length), BF16),
         in_specs=[pl.BlockSpec(memory_space=pl.ANY)] * 9,
         out_specs=pl.BlockSpec(memory_space=pltpu.VMEM),
         scratch_shapes=scratch,

time: 63.4 us -> 61.6 us (0.972)
  local copies, waits for them, and re-layouts: 1.72 us -> 0.73 us
  Pallas kernels: 61.5 us -> 60.8 us
    unnamed x1, local copies, waits for them, and re-layouts: 1.72 us -> 0.73 us
    pallas_call x1, Pallas kernels: 61.5 us -> 60.8 us  [shards(): pl.pallas_call(functools.partial(kernel, sizes), out_shape=pltpu.VMEM((ou...]
where the time goes in v4:
time: 61.6 us; the launch traced here: 61.5 us
  Pallas kernels  60.8 us (99%)
  local copies, waits for them, and re-layouts  0.73 us (1%)
    pallas_call x1, Pallas kernels, shards(): pl.pallas_call(functools.partial(kernel, sizes), out_shape=pltpu.VMEM((ou...  60.8 us

profile of v4, /device:TPU:48, one launch (start us, length us, event | category | flops | bytes accessed | tf_op | source)
XLA Modules:
  0.0 61.5 jit_solution(5108923782382694379)
XLA Ops:
  0.0 60.8 %layer.1 = bf16[320,512]{1,0:T(8,128)(2,1)S(1)} custom-call(bf16[512,640]{1,0:T(8,128)(2,1)} %x_hbm.1, bf16[512,256]{1,0:T(8,128)(2,1)} %bc_hbm.1, f32[4,640]{1,0:T(4,128)} %cx_hbm.1, f32[4,256]{1,0:T(4,128)} %cbc_hbm.1, f32[10,512]{1,0:T(8,128)} %ld_hbm.1, f32[10]{0:T(128)} %d_hbm.1, bf16[512,640]{1,0:T(8,128)(2,1)} %gate_hbm.1, f32[640]{0:T(1024)} %gain_hbm.1, ...), custom_call_target="tpu_custom_call" | custom-call | tf_op jit(solution)/shard_map/layer/pallas_call | solution.py:548
  60.8 0.7 %copy.11 = bf16[512,320]{0,1:T(8,128)(2,1)} copy(bf16[512,320]{0,1:T(8,128)(2,1)S(1)} %bitcast.1) | data formatting | bytes 655360

commit v5 on v4

--- a/solution.py
+++ b/solution.py
@@ -83,6 +83,29 @@
     row_steps = sorted(range(1, nj), key=lambda k: -min(k, nj - k))
     y_steps = sorted(range(1, ny), key=lambda k: -min(k, ny - k))
 
+    def member(index):
+        return {"x": lax.div(index, nc), "c": lax.rem(index, nc)}
+
+    def at(index):
+        return {"y": lax.div(index, nj), **member(lax.rem(index, nj))}
+
+    after = at(lax.rem(flat + 1, ny * nj))
+    ahead = at(lax.rem(flat + ny * nj - 1, ny * nj))
+
+    barrier = pltpu.get_barrier_semaphore()
+
+    def greet(device):
+        pl.semaphore_signal(barrier, inc=1, device_id=device, device_id_type=MESH)
+
+    for k in y_steps:
+        greet({"y": lax.rem(y + k, ny)})
+    greet(after)
+    greet(ahead)
+    for k in row_steps:
+        greet(member(lax.rem(j + k, nj)))
+    for k in range(1, nz):
+        greet({"z": lax.rem(z + k, nz)})
+
     loads = [
         pltpu.make_async_copy(source, target, load_sem.at[i])
         for i, (source, target) in enumerate(
@@ -95,34 +118,13 @@
     for load in loads:
         load.start()
 
-    def member(index):
-        return {"x": lax.div(index, nc), "c": lax.rem(index, nc)}
-
-    def at(index):
-        return {"y": lax.div(index, nj), **member(lax.rem(index, nj))}
-
-    after = at(lax.rem(flat + 1, ny * nj))
-    ahead = at(lax.rem(flat + ny * nj - 1, ny * nj))
-
-    barrier = pltpu.get_barrier_semaphore()
-
-    def greet(device):
-        pl.semaphore_signal(barrier, inc=1, device_id=device, device_id_type=MESH)
-
-    greet(after)
-    greet(ahead)
-    for k in range(1, ny):
-        greet({"y": lax.rem(y + k, ny)})
-    for k in range(1, nz):
-        greet({"z": lax.rem(z + k, nz)})
-    for k in range(1, nj):
-        greet(member(lax.rem(j + k, nj)))
-
+    loads[1].wait()
+    loads[2].wait()
     pl.semaphore_wait(barrier, 2 + (ny - 1) + (nz - 1) + (nj - 1))
     tail = pl.ds(length - 16, 16)
     halos = [
-        remote(x_hbm.at[tail], halo_x, halo_send.at[0], halo_recv.at[0], after),
-        remote(bc_hbm.at[tail], halo_bc, halo_send.at[1], halo_recv.at[1], after),
+        remote(x_in.at[tail], halo_x, halo_send.at[0], halo_recv.at[0], after),
+        remote(bc_in.at[tail], halo_bc, halo_send.at[1], halo_recv.at[1], after),
     ]
 
     @pl.when(flat < ny * nj - 1)
@@ -149,8 +151,8 @@
         copy.start()
         decays.append(copy)
 
-    for load in loads[1:5]:
-        load.wait()
+    loads[3].wait()
+    loads[4].wait()
 
     def filtered(block, taps):
         total = taps[K - 1 : K, :] * block[16:]
@@ -158,17 +160,17 @@
             total = total + taps[tap : tap + 1, :] * pltpu.roll(block, K - 1 - tap, 0)[16:]
         return silu(total).astype(BF16)
 
-    def convolve(here, block_x, block_bc):
-        conv = filtered(block_x.astype(F32), cx)
-        xc[here, :] = conv
-        bcc[here, :] = filtered(block_bc.astype(F32), cbc)
-        weight = jnp.exp(cum[length - 1 : length, :] - cum[here, :])
-        scaled[here, :] = (conv.astype(F32) * weight).astype(BF16)
+    def convolve(here, lanes, block_x):
+        conv = filtered(block_x.astype(F32), cx.at[:, lanes])
+        xc[here, lanes] = conv
+        weight = jnp.exp(cum[length - 1 : length, lanes] - cum[here, lanes])
+        scaled[here, lanes] = (conv.astype(F32) * weight).astype(BF16)
 
     def convolve_at(i, _):
         r = pl.multiple_of(i * ROWS, ROWS)
         block = pl.ds(pl.multiple_of(r - 16, 16), ROWS + 16)
-        convolve(pl.ds(r, ROWS), x_in[block, :], bc_in[block, :])
+        convolve(pl.ds(r, ROWS), slice(0, width), x_in[block, :])
+        bcc[pl.ds(r, ROWS), :] = filtered(bc_in[block, :].astype(F32), cbc)
         return 0
 
     lax.fori_loop(1, length // ROWS, convolve_at, 0)
@@ -184,18 +186,19 @@
         for copy in halos:
             copy.wait_recv()
 
-    convolve(
-        slice(0, ROWS),
-        jnp.concatenate([halo_x[...], x_in[0:ROWS, :]], axis=0),
-        jnp.concatenate([halo_bc[...], bc_in[0:ROWS, :]], axis=0),
-    )
+    begun = slice(0, ROWS)
+    block_bc = jnp.concatenate([halo_bc[...], bc_in[begun, :]], axis=0)
+    bcc[begun, :] = filtered(block_bc.astype(F32), cbc)
 
     def slice_of(index):
         return pl.ds(pl.multiple_of(index * slab, slab), slab)
 
     sent = []
     for half, lanes in enumerate(halves):
-        first = dot(bcc[0:ROWS, 0:N], scaled[0:ROWS, lanes], ((0,), (0,)))
+        convolve(
+            begun, lanes, jnp.concatenate([halo_x[:, lanes], x_in[begun, lanes]], axis=0)
+        )
+        first = dot(bcc[begun, 0:N], scaled[begun, lanes], ((0,), (0,)))
         state[:, lanes] = (later[:, lanes] + first).astype(BF16)
         for k in row_steps:
             other = lax.rem(j + k, nj)
@@ -262,7 +265,7 @@
             ya[t, lanes] = jnp.where(left, results[0], results[1]) + skip * xc[t, lanes].astype(F32)
         return 0
 
-    lax.fori_loop(0, 2, local_pair, 0)
+    lax.fori_loop(0, 3, local_pair, 0)
 
     def y_copy(half, k):
         lanes = halves[half]
@@ -290,8 +293,9 @@
             def _(half=half, k=k):
                 y_copy(half, k).start()
 
-    lax.fori_loop(2, pairs, local_pair, 0)
-
+    n_blocks = length // ROWS
+    pairs_first = jnp.where(y >= 3, pairs, 3)
+    gates_first = jnp.where(y >= 3, n_blocks, 0)
     loads[6].wait()
 
     def gates(i, _):
@@ -301,17 +305,8 @@
         yb[here, :] = jnp.exp(cum[here, :]) * factor
         return 0
 
-    lax.fori_loop(0, length // ROWS, gates, 0)
-
-    loads[8].wait()
-
-    def turn(i, _):
-        here = pl.ds(pl.multiple_of(i * LANES, LANES), LANES)
-        wt[here, :] = w[:, here].T
-        return 0
-
-    blocks = w.shape[1] // LANES
-    lax.fori_loop(0, blocks * 5 // 8, turn, 0)
+    lax.fori_loop(3, pairs_first, local_pair, 0)
+    lax.fori_loop(0, gates_first, gates, 0)
 
     for k in range(1, ny):
         other = lax.rem(y + k, ny)
@@ -350,8 +345,32 @@
             returned.append(copy)
         carried[slice_of(j), lanes] = c_out[j, :, lanes]
 
+    lax.fori_loop(pairs_first, pairs, local_pair, 0)
+    lax.fori_loop(gates_first, n_blocks, gates, 0)
+
+    rows_out = out_ref.shape[0]
+    sign = 1 - 2 * c
+    n_long = nz // 2
+    n_short = n_long - 1
+
+    def towards(offset):
+        return lax.rem(z + offset * sign + 2 * nz, nz)
+
+    def turn(d):
+        begin = lax.div(d * rows_out, LANES)
+
+        def turn_block(i, _):
+            here = pl.ds(pl.multiple_of((begin + i) * LANES, LANES), LANES)
+            wt[here, :] = w[:, here].T
+            return 0
+
+        lax.fori_loop(0, pl.cdiv(rows_out, LANES), turn_block, 0)
+
+    loads[8].wait()
+    turn(towards(n_long))
+    if n_short:
+        turn(towards(-n_short))
     loads[7].wait()
-    lax.fori_loop(blocks * 5 // 8, blocks, turn, 0)
     amount = gain[...].reshape(1, width)
 
     def await_carried(half):
@@ -380,7 +399,6 @@
     await_carried(0)
     lax.fori_loop(0, length // LANES, finish_first, 0)
 
-    rows_out = out_ref.shape[0]
     piece = length // SUBS
 
     def tokens(q):
@@ -395,13 +413,6 @@
         part = dot(wt[here, :], ut[...], ((1,), (0,))).astype(BF16)
         for q in range(SUBS):
             chunks[d, q] = part[:, q * piece : (q + 1) * piece]
-
-    sign = 1 - 2 * c
-    n_long = nz // 2
-    n_short = n_long - 1
-
-    def towards(offset):
-        return lax.rem(z + offset * sign + 2 * nz, nz)
 
     def long_copy(source, step, q):
         return remote(
@@ -439,13 +450,18 @@
         copy.start()
         shared.append(copy)
 
+    def turn_and_project(d):
+        turn(d)
+        project(d)
+
+    if n_long == 1:
+        turn_and_project(z)
     for step in range(1, n_long):
-        project(towards(n_long - step))
+        turn_and_project(towards(n_long - step))
         if step < n_short:
-            project(towards(step - n_short))
-    project(z)
-
-    for step in range(1, n_long):
+            turn_and_project(towards(step - n_short))
+        if step == n_long - 1:
+            turn_and_project(z)
 
         def relay(q, _, step=step):
             long_copy(long_in.at[step - 1, q], step - 1, q).wait_recv()

time: 61.6 us -> 61.3 us (level)
  no operation moved by 1% of the time
where the time goes in v5:
time: 61.3 us; the launch traced here: 61.2 us
  Pallas kernels  60.5 us (99%)
  local copies, waits for them, and re-layouts  0.73 us (1%)
    pallas_call x1, Pallas kernels, shards(): pl.pallas_call(functools.partial(kernel, sizes), out_shape=pltpu.VMEM((ou...  60.5 us

profile of v5, /device:TPU:48, one launch (start us, length us, event | category | flops | bytes accessed | tf_op | source)
XLA Modules:
  0.0 61.2 jit_solution(12210579425273166706)
XLA Ops:
  0.0 60.5 %layer.1 = bf16[320,512]{1,0:T(8,128)(2,1)S(1)} custom-call(bf16[512,640]{1,0:T(8,128)(2,1)} %x_hbm.1, bf16[512,256]{1,0:T(8,128)(2,1)} %bc_hbm.1, f32[4,640]{1,0:T(4,128)} %cx_hbm.1, f32[4,256]{1,0:T(4,128)} %cbc_hbm.1, f32[10,512]{1,0:T(8,128)} %ld_hbm.1, f32[10]{0:T(128)} %d_hbm.1, bf16[512,640]{1,0:T(8,128)(2,1)} %gate_hbm.1, f32[640]{0:T(1024)} %gain_hbm.1, ...), custom_call_target="tpu_custom_call" | custom-call | tf_op jit(solution)/shard_map/layer/pallas_call | solution.py:564
  60.5 0.7 %copy.11 = bf16[512,320]{0,1:T(8,128)(2,1)} copy(bf16[512,320]{0,1:T(8,128)(2,1)S(1)} %bitcast.1) | data formatting | bytes 655360

commit v6 on v5

--- a/solution.py
+++ b/solution.py
@@ -78,7 +78,7 @@
     heads, length = ld.shape
     width = x_in.shape[1]
     pairs = width // LANES
-    cut = (pairs + 1) // 2 * LANES
+    cut = pairs // 2 * LANES
     halves = [slice(0, cut), slice(cut, width)]
     row_steps = sorted(range(1, nj), key=lambda k: -min(k, nj - k))
     y_steps = sorted(range(1, ny), key=lambda k: -min(k, ny - k))

time: 61.3 us -> 61.1 us (level)
  no operation moved by 1% of the time
where the time goes in v6:
time: 61.1 us; the launch traced here: 61 us
  Pallas kernels  60.2 us (99%)
  local copies, waits for them, and re-layouts  0.73 us (1%)
    pallas_call x1, Pallas kernels, shards(): pl.pallas_call(functools.partial(kernel, sizes), out_shape=pltpu.VMEM((ou...  60.2 us

profile of v6, /device:TPU:48, one launch (start us, length us, event | category | flops | bytes accessed | tf_op | source)
XLA Modules:
  0.0 61.0 jit_solution(6415895809739319420)
XLA Ops:
  0.0 60.2 %layer.1 = bf16[320,512]{1,0:T(8,128)(2,1)S(1)} custom-call(bf16[512,640]{1,0:T(8,128)(2,1)} %x_hbm.1, bf16[512,256]{1,0:T(8,128)(2,1)} %bc_hbm.1, f32[4,640]{1,0:T(4,128)} %cx_hbm.1, f32[4,256]{1,0:T(4,128)} %cbc_hbm.1, f32[10,512]{1,0:T(8,128)} %ld_hbm.1, f32[10]{0:T(128)} %d_hbm.1, bf16[512,640]{1,0:T(8,128)(2,1)} %gate_hbm.1, f32[640]{0:T(1024)} %gain_hbm.1, ...), custom_call_target="tpu_custom_call" | custom-call | tf_op jit(solution)/shard_map/layer/pallas_call | solution.py:564
  60.3 0.7 %copy.11 = bf16[512,320]{0,1:T(8,128)(2,1)} copy(bf16[512,320]{0,1:T(8,128)(2,1)S(1)} %bitcast.1) | data formatting | bytes 655360
